TPU v7x, 32 devices: a whole 2x2x4 slice. The times are simulated.
32 devices in a mesh: expert: 16 (over z, x, core), shard: 2 (over y).
Axes of the slice: x: 2, y: 2, z: 4, core: 2. Of those that a mesh axis runs over, the one named last changes fastest.
Arguments:
- tokens: bfloat16 [4096, 2048], P(('expert', 'shard')), may hold values from -6 to 6
- segment_ids: int32 [32, 128], P(('expert', 'shard')), may hold values from 0 to 3, never falling along the last dimension, each value on 1 to 64 neighbouring positions
- routes: int32 [4096, 6], P(('expert', 'shard')), may hold values from 0 to 15, all different within a row; in each aligned block of 128 rows (0 to 127, 128 to 255, ...) at most 96 rows name the same one
- attn_gain: bfloat16 [2048], P('shard'), may hold values from 0.5 to 1.5
- w_query: bfloat16 [2048, 3072], P('shard'), may hold values from -0.125 to 0.125
- w_latent: bfloat16 [2048, 576], P('shard'), may hold values from -0.125 to 0.125
- latent_gain: bfloat16 [512], P('shard'), may hold values from 0.5 to 1.5
- w_keyval: bfloat16 [512, 4096], P('shard'), may hold values from -0.25 to 0.25
- w_output: bfloat16 [2048, 2048], P('shard'), may hold values from -0.5 to 0.5
- ffn_gain: bfloat16 [2048], P('shard'), may hold values from 0.5 to 1.5
- w_router: bfloat16 [2048, 16], P('shard'), may hold values from -0.125 to 0.125
- shared_gate: bfloat16 [2048, 1408], P('shard'), may hold values from -0.125 to 0.125
- shared_up: bfloat16 [2048, 1408], P('shard'), may hold values from -0.125 to 0.125
- shared_down: bfloat16 [1408, 2048], P('shard'), may hold values from -0.15625 to 0.15625
- expert_gate: bfloat16 [16, 2048, 1408], P('expert', None, 'shard'), may hold values from -0.125 to 0.125
- expert_up: bfloat16 [16, 2048, 1408], P('expert', None, 'shard'), may hold values from -0.125 to 0.125
- expert_down: bfloat16 [16, 1408, 2048], P('expert', 'shard'), may hold values from -0.15625 to 0.15625
- cotangent: bfloat16 [4096, 2048], P(('expert', 'shard')), may hold values from -6 to 6
Outputs:
- block_out: bfloat16 [4096, 2048], P(('expert', 'shard'))
- tokens_grad: float32 [4096, 2048], P(('expert', 'shard'))
- attn_gain_grad: float32 [2048], P('shard')
- w_query_grad: float32 [2048, 3072], P('shard')
- w_latent_grad: float32 [2048, 576], P('shard')
- latent_gain_grad: float32 [512], P('shard')
- w_keyval_grad: float32 [512, 4096], P('shard')
- w_output_grad: float32 [2048, 2048], P('shard')
- ffn_gain_grad: float32 [2048], P('shard')
- w_router_grad: float32 [2048, 16], P('shard')
- shared_gate_grad: float32 [2048, 1408], P('shard')
- shared_up_grad: float32 [2048, 1408], P('shard')
- shared_down_grad: float32 [1408, 2048], P('shard')
- expert_gate_grad: float32 [16, 2048, 1408], P('expert', None, 'shard')
- expert_up_grad: float32 [16, 2048, 1408], P('expert', None, 'shard')
- expert_down_grad: float32 [16, 1408, 2048], P('expert', 'shard')
Inputs may be any that keep to these rules, and one draw needn't show every extreme that they name: `segment_ids`: within each row the document numbers never fall; a document holds 1 to 64 tokens, and some document holds exactly 64. `routes`: A token's 6 experts differ; among the 128 tokens of one device no expert is named more than 96 times, and in some device some expert is named exactly 96 times.
All inputs are finite; a program needn't handle non-finite values.
Results may differ from a plain program's by a relative error of at most 0.019.
Values may be sent and summed in bfloat16 or wider, within the bound.
No kernel may reach another device: no remote copies, remote signals or barrier semaphores. Data moves between devices by JAX's collectives and lax.ppermute only.
A program may use at most 512 MiB of HBM per device.

v0:
```python
import jax
import jax.numpy as jnp
from jax import lax
from jax.sharding import PartitionSpec as P

HEADS = 16
NOPE = 128
ROPE = 64
VDIM = 128
KVR = 512


NORM_EPSILON = 1e-06
ROTARY_BASE = 50000.0
ROUTE_SCALE = 2.446
NEGATIVE = -1e30


def norm_scale(values):
    return lax.rsqrt(jnp.mean(values * values, axis=-1, keepdims=True) + NORM_EPSILON)


def norm_backward(upstream, values, scale_row, gain_row):
    normed = values * scale_row
    gain_grad = jnp.sum(upstream * normed, axis=0)
    inner_grad = upstream * gain_row
    values_grad = scale_row * (
        inner_grad - normed * jnp.mean(inner_grad * normed, axis=-1, keepdims=True)
    )
    return (values_grad, gain_grad)


def lead_product(former, latter):
    return lax.dot_general(
        former, latter, (((0,), (0,)), ((), ())), preferred_element_type=jnp.float32
    )


def trail_product(former, latter):
    return lax.dot_general(
        former, latter, (((1,), (1,)), ((), ())), preferred_element_type=jnp.float32
    )


def plain_product(former, latter):
    return jnp.dot(former, latter, preferred_element_type=jnp.float32)


def batched(pattern, former, latter):
    return jnp.einsum(pattern, former, latter, preferred_element_type=jnp.float32)


def rotary_tables(segment_row):
    length = segment_row.shape[0]
    places = jnp.arange(length, dtype=jnp.int32)
    same_document = segment_row[:, None] == segment_row[None, :]
    position = jnp.sum(
        jnp.where(same_document & (places[None, :] < places[:, None]), 1.0, 0.0), axis=1
    )
    half_rope = ROPE // 2
    frequency = ROTARY_BASE ** (-2.0 * jnp.arange(half_rope, dtype=jnp.float32) / ROPE)
    angles = position[:, None] * frequency[None, :]
    cosine = jnp.concatenate([jnp.cos(angles), jnp.cos(angles)], axis=1)
    sine_table = jnp.concatenate([jnp.sin(angles), jnp.sin(angles)], axis=1)
    allowed = same_document & (places[None, :] <= places[:, None])
    return (cosine, sine_table, allowed)


def rotate(values, cosine, sine_table):
    half_rope = values.shape[-1] // 2
    turned = jnp.concatenate([-values[..., half_rope:], values[..., :half_rope]], axis=-1)
    return values * cosine + turned * sine_table


def unrotate(upstream, cosine, sine_table):
    half_rope = upstream.shape[-1] // 2
    weighted = upstream * sine_table
    turned = jnp.concatenate([weighted[..., half_rope:], -weighted[..., :half_rope]], axis=-1)
    return upstream * cosine + turned


def attention_scores(query_b, key_b, allowed):
    scores = batched("thd,shd->hts", query_b, key_b) * (NOPE + ROPE) ** (-0.5)
    return jnp.where(allowed[None, :, :], scores, NEGATIVE)


def attend_forward(inputs, segment_row, weights):
    attn_gain, w_query, w_latent, latent_gain, w_keyval, w_output = weights
    row_count = inputs.shape[0]
    cosine, sine_table, allowed = rotary_tables(segment_row)
    scale_one = norm_scale(inputs)
    normed_one = (inputs * scale_one * attn_gain.astype(jnp.float32)).astype(jnp.bfloat16)
    queries = plain_product(normed_one, w_query).reshape(row_count, HEADS, NOPE + ROPE)
    query_turn = rotate(queries[:, :, NOPE:], cosine[:, None, :], sine_table[:, None, :])
    query_b = jnp.concatenate([queries[:, :, :NOPE], query_turn], axis=-1).astype(jnp.bfloat16)
    latent_all = plain_product(normed_one, w_latent)
    latent = latent_all[:, :KVR]
    key_rope = rotate(latent_all[:, KVR:], cosine, sine_table)
    scale_latent = norm_scale(latent)
    latent_normed = (latent * scale_latent * latent_gain.astype(jnp.float32)).astype(jnp.bfloat16)
    keyval = plain_product(latent_normed, w_keyval).reshape(row_count, HEADS, NOPE + VDIM)
    key_shared = jnp.broadcast_to(key_rope[:, None, :], (row_count, HEADS, ROPE))
    key_b = jnp.concatenate([keyval[:, :, :NOPE], key_shared], axis=-1).astype(jnp.bfloat16)
    value_b = keyval[:, :, NOPE:].astype(jnp.bfloat16)
    scores = attention_scores(query_b, key_b, allowed)
    peak_score = jnp.max(scores, axis=-1, keepdims=True)
    raised = jnp.exp(scores - peak_score)
    totals = jnp.sum(raised, axis=-1, keepdims=True)
    probs_b = (raised / totals).astype(jnp.bfloat16)
    log_total = peak_score + jnp.log(totals)
    attended = (
        batched("hts,shd->thd", probs_b, value_b)
        .astype(jnp.bfloat16)
        .reshape(row_count, HEADS * VDIM)
    )
    residual = inputs + plain_product(attended, w_output)
    return {
        "inputs": inputs,
        "scale_one": scale_one,
        "normed_one": normed_one,
        "latent": latent,
        "scale_latent": scale_latent,
        "latent_normed": latent_normed,
        "query_b": query_b,
        "key_b": key_b,
        "value_b": value_b,
        "log_total": log_total,
        "attended": attended,
        "cosine": cosine,
        "sine_table": sine_table,
        "allowed": allowed,
        "residual": residual,
    }


def attend_backward(residual_grad, saved, weights):
    attn_gain, w_query, w_latent, latent_gain, w_keyval, w_output = weights
    row_count = residual_grad.shape[0]
    grad_b = residual_grad.astype(jnp.bfloat16)
    attended_grad = (
        trail_product(grad_b, w_output).astype(jnp.bfloat16).reshape(row_count, HEADS, VDIM)
    )
    scores = attention_scores(saved["query_b"], saved["key_b"], saved["allowed"])
    probabilities = jnp.exp(scores - saved["log_total"])
    value_grad = batched("hts,thd->shd", probabilities.astype(jnp.bfloat16), attended_grad)
    probs_grad = batched("thd,shd->hts", attended_grad, saved["value_b"])
    center = jnp.sum(probabilities * probs_grad, axis=-1, keepdims=True)
    scores_grad = (probabilities * (probs_grad - center) * (NOPE + ROPE) ** (-0.5)).astype(
        jnp.bfloat16
    )
    query_grad = batched("hts,shd->thd", scores_grad, saved["key_b"])
    key_grad = batched("hts,thd->shd", scores_grad, saved["query_b"])
    cosine = saved["cosine"]
    sine_table = saved["sine_table"]
    query_turn_grad = unrotate(query_grad[:, :, NOPE:], cosine[:, None, :], sine_table[:, None, :])
    query_grad_b = (
        jnp.concatenate([query_grad[:, :, :NOPE], query_turn_grad], axis=-1)
        .astype(jnp.bfloat16)
        .reshape(row_count, HEADS * (NOPE + ROPE))
    )
    normed_grad = trail_product(query_grad_b, w_query)
    key_rope_grad = unrotate(jnp.sum(key_grad[:, :, NOPE:], axis=1), cosine, sine_table)
    keyval_grad_b = (
        jnp.concatenate([key_grad[:, :, :NOPE], value_grad], axis=-1)
        .astype(jnp.bfloat16)
        .reshape(row_count, HEADS * (NOPE + VDIM))
    )
    latent_normed_grad = trail_product(keyval_grad_b, w_keyval)
    latent_grad, latent_gain_grad = norm_backward(
        latent_normed_grad, saved["latent"], saved["scale_latent"], latent_gain.astype(jnp.float32)
    )
    latent_all_grad = jnp.concatenate([latent_grad, key_rope_grad], axis=-1).astype(jnp.bfloat16)
    normed_grad = normed_grad + trail_product(latent_all_grad, w_latent)
    inputs_grad, attn_gain_grad = norm_backward(
        normed_grad, saved["inputs"], saved["scale_one"], attn_gain.astype(jnp.float32)
    )
    factors = (
        saved["normed_one"],
        query_grad_b,
        latent_all_grad,
        saved["latent_normed"],
        keyval_grad_b,
        saved["attended"],
        grad_b,
    )
    return (residual_grad + inputs_grad, (attn_gain_grad, latent_gain_grad), factors)


def route_gates(normed_two, route_rows, router_full):
    expert_total = router_full.shape[1]
    scores = jax.nn.sigmoid(plain_product(normed_two, router_full))
    chosen_mask = route_rows[:, :, None] == jnp.arange(expert_total, dtype=jnp.int32)[None, None, :]
    picked = jnp.sum(jnp.where(chosen_mask, scores[:, None, :], 0.0), axis=2)
    gate_values = ROUTE_SCALE * picked / jnp.sum(picked, axis=1, keepdims=True)
    return (gate_values, picked, chosen_mask)


def body(
    tokens,
    segment_ids,
    routes,
    attn_gain,
    w_query,
    w_latent,
    latent_gain,
    w_keyval,
    w_output,
    ffn_gain,
    w_router,
    shared_gate,
    shared_up,
    shared_down,
    expert_gate,
    expert_up,
    expert_down,
    cotangent,
):
    token_count = tokens.shape[0]
    model_width = tokens.shape[1]
    route_count = routes.shape[1]
    owners = lax.axis_size("expert")
    gathered = (
        lax.all_gather(attn_gain, "shard", axis=0, tiled=True),
        lax.all_gather(w_query, "shard", axis=0, tiled=True),
        lax.all_gather(w_latent, "shard", axis=0, tiled=True),
        lax.all_gather(latent_gain, "shard", axis=0, tiled=True),
        lax.all_gather(w_keyval, "shard", axis=0, tiled=True),
        lax.all_gather(w_output, "shard", axis=0, tiled=True),
        lax.all_gather(ffn_gain, "shard", axis=0, tiled=True),
        lax.all_gather(w_router, "shard", axis=0, tiled=True),
        lax.all_gather(shared_gate, "shard", axis=0, tiled=True),
        lax.all_gather(shared_up, "shard", axis=0, tiled=True),
        lax.all_gather(shared_down, "shard", axis=0, tiled=True),
    )
    attn_full = gathered[:6]
    ffn_full = gathered[6]
    router_full = gathered[7]
    shared_gate_full = gathered[8]
    shared_up_full = gathered[9]
    shared_down_full = gathered[10]
    expert_total = router_full.shape[1]
    capacity = min(token_count, 2 * token_count * route_count // expert_total)
    inputs = tokens.astype(jnp.float32)
    saved = attend_forward(inputs, segment_ids[0], attn_full)
    residual = saved["residual"]
    scale_two = norm_scale(residual)
    normed_two = (residual * scale_two * ffn_full.astype(jnp.float32)).astype(jnp.bfloat16)
    gate_values, picked, chosen_mask = route_gates(normed_two, routes, router_full)
    flat_routes = routes.reshape(-1)
    flat_count = flat_routes.shape[0]
    onehot = (flat_routes[:, None] == jnp.arange(expert_total, dtype=jnp.int32)[None, :]).astype(
        jnp.int32
    )
    slot_rank = jnp.sum((jnp.cumsum(onehot, axis=0) - 1) * onehot, axis=1)
    slot_index = flat_routes * capacity + slot_rank
    source_row = (
        jnp.full((expert_total * capacity,), flat_count, jnp.int32)
        .at[slot_index]
        .set(jnp.arange(flat_count, dtype=jnp.int32))
    )
    normed_padded = jnp.concatenate([normed_two, jnp.zeros((1, model_width), jnp.bfloat16)], axis=0)
    send_rows = normed_padded[source_row // route_count].reshape(
        expert_total, capacity, model_width
    )
    arrived = lax.all_to_all(send_rows, "expert", split_axis=0, concat_axis=0, tiled=True)
    owner_rows = lax.all_gather(
        arrived.reshape(owners * capacity, model_width), "shard", axis=0, tiled=True
    )
    gate_local = expert_gate[0]
    up_local = expert_up[0]
    down_local = expert_down[0]
    pre_gate = plain_product(owner_rows, gate_local)
    pre_up = plain_product(owner_rows, up_local)
    sig_gate = jax.nn.sigmoid(pre_gate)
    hidden = (pre_gate * sig_gate * pre_up).astype(jnp.bfloat16)
    expert_sum = lax.psum_scatter(
        plain_product(hidden, down_local).astype(jnp.bfloat16),
        "shard",
        scatter_dimension=0,
        tiled=True,
    )
    returned = lax.all_to_all(
        expert_sum.reshape(owners, capacity, model_width),
        "expert",
        split_axis=0,
        concat_axis=0,
        tiled=True,
    )
    chosen_out = (
        returned.reshape(expert_total * capacity, model_width)[slot_index]
        .reshape(token_count, route_count, model_width)
        .astype(jnp.float32)
    )
    routed = jnp.sum(gate_values[:, :, None] * chosen_out, axis=1)
    shared_pre_gate = plain_product(normed_two, shared_gate_full)
    shared_pre_up = plain_product(normed_two, shared_up_full)
    shared_sig = jax.nn.sigmoid(shared_pre_gate)
    shared_hidden = (shared_pre_gate * shared_sig * shared_pre_up).astype(jnp.bfloat16)
    block_out = (residual + routed + plain_product(shared_hidden, shared_down_full)).astype(
        jnp.bfloat16
    )
    upstream = cotangent.astype(jnp.float32)
    gate_grads = jnp.sum(upstream[:, None, :] * chosen_out, axis=2)
    grad_rows = (
        (gate_values[:, :, None] * upstream[:, None, :])
        .astype(jnp.bfloat16)
        .reshape(flat_count, model_width)
    )
    grad_padded = jnp.concatenate([grad_rows, jnp.zeros((1, model_width), jnp.bfloat16)], axis=0)
    send_grads = grad_padded[source_row].reshape(expert_total, capacity, model_width)
    arrived_grads = lax.all_to_all(send_grads, "expert", split_axis=0, concat_axis=0, tiled=True)
    owner_grads = lax.all_gather(
        arrived_grads.reshape(owners * capacity, model_width), "shard", axis=0, tiled=True
    )
    down_grad = lead_product(hidden, owner_grads)
    hidden_grad = trail_product(owner_grads, down_local)
    pre_gate_grad = (hidden_grad * pre_up * sig_gate * (1.0 + pre_gate * (1.0 - sig_gate))).astype(
        jnp.bfloat16
    )
    pre_up_grad = (hidden_grad * pre_gate * sig_gate).astype(jnp.bfloat16)
    gate_w_grad = lead_product(owner_rows, pre_gate_grad)
    up_w_grad = lead_product(owner_rows, pre_up_grad)
    input_sum = lax.psum_scatter(
        (trail_product(pre_gate_grad, gate_local) + trail_product(pre_up_grad, up_local)).astype(
            jnp.bfloat16
        ),
        "shard",
        scatter_dimension=0,
        tiled=True,
    )
    back_grads = lax.all_to_all(
        input_sum.reshape(owners, capacity, model_width),
        "expert",
        split_axis=0,
        concat_axis=0,
        tiled=True,
    )
    chosen_grads = back_grads.reshape(expert_total * capacity, model_width)[slot_index].reshape(
        token_count, route_count, model_width
    )
    normed_two_grad = jnp.sum(chosen_grads.astype(jnp.float32), axis=1)
    backward_weights = (
        lax.all_gather(attn_gain, "shard", axis=0, tiled=True),
        lax.all_gather(w_query, "shard", axis=0, tiled=True),
        lax.all_gather(w_latent, "shard", axis=0, tiled=True),
        lax.all_gather(latent_gain, "shard", axis=0, tiled=True),
        lax.all_gather(w_keyval, "shard", axis=0, tiled=True),
        lax.all_gather(w_output, "shard", axis=0, tiled=True),
        lax.all_gather(ffn_gain, "shard", axis=0, tiled=True),
        lax.all_gather(w_router, "shard", axis=0, tiled=True),
        lax.all_gather(shared_gate, "shard", axis=0, tiled=True),
        lax.all_gather(shared_up, "shard", axis=0, tiled=True),
        lax.all_gather(shared_down, "shard", axis=0, tiled=True),
    )
    attn_back = backward_weights[:6]
    ffn_back = backward_weights[6]
    router_back = backward_weights[7]
    shared_gate_back = backward_weights[8]
    shared_up_back = backward_weights[9]
    shared_down_back = backward_weights[10]
    shared_hidden_grad = trail_product(cotangent, shared_down_back)
    shared_gate_pre_grad = (
        shared_hidden_grad
        * shared_pre_up
        * shared_sig
        * (1.0 + shared_pre_gate * (1.0 - shared_sig))
    ).astype(jnp.bfloat16)
    shared_up_pre_grad = (shared_hidden_grad * shared_pre_gate * shared_sig).astype(jnp.bfloat16)
    normed_two_grad = (
        normed_two_grad
        + trail_product(shared_gate_pre_grad, shared_gate_back)
        + trail_product(shared_up_pre_grad, shared_up_back)
    )
    picked_total = jnp.sum(picked, axis=1, keepdims=True)
    weighted = jnp.sum(gate_grads * picked, axis=1, keepdims=True)
    picked_grad = ROUTE_SCALE * (
        gate_grads / picked_total - weighted / (picked_total * picked_total)
    )
    logit_pick = picked_grad * picked * (1.0 - picked)
    logit_grad_b = jnp.sum(jnp.where(chosen_mask, logit_pick[:, :, None], 0.0), axis=1).astype(
        jnp.bfloat16
    )
    normed_two_grad = normed_two_grad + trail_product(logit_grad_b, router_back)
    residual_norm_grad, ffn_gain_grad = norm_backward(
        normed_two_grad, residual, scale_two, ffn_back.astype(jnp.float32)
    )
    residual_grad = upstream + residual_norm_grad
    tokens_grad, attn_gains, factors = attend_backward(residual_grad, saved, attn_back)
    attn_gain_grad, latent_gain_grad = attn_gains
    normed_one, query_grad_b, latent_all_grad, latent_normed, keyval_grad_b, attended, grad_b = (
        factors
    )
    collected = (
        lax.all_gather(normed_one, "shard", axis=0, tiled=True),
        lax.all_gather(query_grad_b, "shard", axis=0, tiled=True),
        lax.all_gather(latent_all_grad, "shard", axis=0, tiled=True),
        lax.all_gather(latent_normed, "shard", axis=0, tiled=True),
        lax.all_gather(keyval_grad_b, "shard", axis=0, tiled=True),
        lax.all_gather(attended, "shard", axis=0, tiled=True),
        lax.all_gather(grad_b, "shard", axis=0, tiled=True),
        lax.all_gather(normed_two, "shard", axis=0, tiled=True),
        lax.all_gather(logit_grad_b, "shard", axis=0, tiled=True),
        lax.all_gather(shared_gate_pre_grad, "shard", axis=0, tiled=True),
        lax.all_gather(shared_up_pre_grad, "shard", axis=0, tiled=True),
        lax.all_gather(shared_hidden, "shard", axis=0, tiled=True),
        lax.all_gather(cotangent, "shard", axis=0, tiled=True),
    )
    group_size = lax.axis_size("shard")
    shard_place = lax.axis_index("shard")

    def slice_product(former, latter):
        own_rows = former.shape[1] // group_size
        own_piece = lax.dynamic_slice_in_dim(former, shard_place * own_rows, own_rows, 1)
        return lead_product(own_piece, latter)

    gain_shares = (
        lax.psum_scatter(attn_gain_grad, "shard", scatter_dimension=0, tiled=True),
        lax.psum_scatter(latent_gain_grad, "shard", scatter_dimension=0, tiled=True),
        lax.psum_scatter(ffn_gain_grad, "shard", scatter_dimension=0, tiled=True),
    )
    shares = (
        gain_shares[0],
        slice_product(collected[0], collected[1]),
        slice_product(collected[0], collected[2]),
        gain_shares[1],
        slice_product(collected[3], collected[4]),
        slice_product(collected[5], collected[6]),
        gain_shares[2],
        slice_product(collected[7], collected[8]),
        slice_product(collected[7], collected[9]),
        slice_product(collected[7], collected[10]),
        slice_product(collected[11], collected[12]),
    )
    totals = lax.psum(
        (
            shares[0],
            shares[1],
            shares[2],
            shares[3],
            shares[4],
            shares[5],
            shares[6],
            shares[7],
            shares[8],
            shares[9],
            shares[10],
        ),
        "expert",
    )
    return (
        block_out,
        tokens_grad,
        totals[0],
        totals[1],
        totals[2],
        totals[3],
        totals[4],
        totals[5],
        totals[6],
        totals[7],
        totals[8],
        totals[9],
        totals[10],
        gate_w_grad[None],
        up_w_grad[None],
        down_grad[None],
    )


def solution(mesh):
    in_specs = (
        P(("expert", "shard"), None),
        P(("expert", "shard"), None),
        P(("expert", "shard"), None),
        P("shard"),
        P("shard", None),
        P("shard", None),
        P("shard"),
        P("shard", None),
        P("shard", None),
        P("shard"),
        P("shard", None),
        P("shard", None),
        P("shard", None),
        P("shard", None),
        P("expert", None, "shard"),
        P("expert", None, "shard"),
        P("expert", "shard", None),
        P(("expert", "shard"), None),
    )
    out_specs = (
        P(("expert", "shard"), None),
        P(("expert", "shard"), None),
        P("shard"),
        P("shard", None),
        P("shard", None),
        P("shard"),
        P("shard", None),
        P("shard", None),
        P("shard"),
        P("shard", None),
        P("shard", None),
        P("shard", None),
        P("shard", None),
        P("expert", None, "shard"),
        P("expert", None, "shard"),
        P("expert", "shard", None),
    )
    return jax.shard_map(body, mesh=mesh, in_specs=in_specs, out_specs=out_specs, check_vma=False)
```

profile of v0, /device:TPU:0, one launch (start us, length us, event | category | flops | bytes accessed | tf_op | source)
XLA Modules:
  0.0 2419.2 jit_solution(7445436615145864986)
XLA Ops:
  34.4 14.0 all-gather.18.cloned.1.call-done
  52.0 54.7 %all-gather.20.cloned.1.call-done = bf16[512,4096]{1,0:T(8,128)(2,1)} async-done(((bf16[256,4096]{1,0:T(8,128)(2,1)}), bf16[512,4096]{1,0:T(8,128)(2,1)}) %all-gather.20.cloned.1.call-update) | async-done | bytes 4194320 | tf_op jit(solution)/shard_map/all_gather | solution.py:227
  114.8 146.1 %all-gather.22.cloned.1.call-done = bf16[2048,3072]{1,0:T(8,128)(2,1)} async-done(((bf16[1024,3072]{1,0:T(8,128)(2,1)}), bf16[2048,3072]{1,0:T(8,128)(2,1)}) %all-gather.22.cloned.1.call-update) | async-done | bytes 12582928 | tf_op jit(solution)/shard_map/all_gather | solution.py:224
  260.9 8.2 fusion.101
  272.9 93.4 %all-gather.24.cloned.1.call-done = bf16[2048,2048]{1,0:T(8,128)(2,1)} async-done(((bf16[1024,2048]{1,0:T(8,128)(2,1)}), bf16[2048,2048]{1,0:T(8,128)(2,1)}) %all-gather.24.cloned.1.call-update) | async-done | bytes 8388624 | tf_op jit(solution)/shard_map/all_gather | solution.py:228
  374.3 7.0 gather_fusion
  381.2 5.8 all-to-all-start
  391.7 8.3 mul.410
  405.3 95.9 %all-to-all-done = bf16[16,96,2048]{2,1,0:T(8,128)(2,1)} async-done(((bf16[16,96,2048]{2,1,0:T(8,128)(2,1)}), bf16[16,96,2048]{2,1,0:T(8,128)(2,1)}, u32[]{:S(2)}, u32[]{:S(2)}) %all-to-all-start) | async-done | bytes 6291488 | tf_op jit(solution)/shard_map/all_to_all | solution.py:265
  506.9 15.0 gather_fusion.2
  521.8 166.0 %all_to_all.20 = bf16[16,96,2048]{2,1,0:T(8,128)(2,1)} all-to-all(bf16[16,96,2048]{2,1,0:T(8,128)(2,1)} %bitcast.122), channel_id=1, replica_groups=mesh['expert'=16,'shard'=2] {'expert'}, dimensions={0} | all-to-all | bytes 12582912 | tf_op jit(solution)/shard_map/all_to_all | solution.py:311
  688.0 15.8 fusion.5
  703.8 11.4 fusion.9
  715.3 125.2 %all-gather.34.cloned.1.call-done = bf16[3072,2048]{1,0:T(8,128)(2,1)} async-done(((bf16[1536,2048]{1,0:T(8,128)(2,1)}), bf16[3072,2048]{1,0:T(8,128)(2,1)}) %all-gather.34.cloned.1.call-update) | async-done | bytes 12582928 | tf_op jit(solution)/shard_map/all_gather | solution.py:312
  840.5 22.4 multiply_convert_fusion
  862.8 14.6 convolution_convert_fusion
  879.3 16.0 fusion.7
  895.2 19.2 add_convert_fusion
  915.3 106.8 %reduce-scatter.3.cloned.1.call-done = bf16[1536,2048]{1,0:T(8,128)(2,1)} async-done(((bf16[3072,2048]{1,0:T(8,128)(2,1)}), bf16[1536,2048]{1,0:T(8,128)(2,1)}) %reduce-scatter.3.cloned.1.call-update) | async-done | bytes 6291472 | tf_op jit(solution)/shard_map/reduce_scatter | solution.py:276
  1022.1 5.7 all-to-all-start.1
  1029.1 139.8 %reduce-scatter.5.cloned.1.call-done = bf16[1536,2048]{1,0:T(8,128)(2,1)} async-done(((bf16[3072,2048]{1,0:T(8,128)(2,1)}), bf16[1536,2048]{1,0:T(8,128)(2,1)}) %reduce-scatter.5.cloned.1.call-update) | async-done | bytes 6291472 | tf_op jit(solution)/shard_map/reduce_scatter | solution.py:323
  1168.9 5.8 all-to-all-start.3
  1176.8 7.2 all_gather.105
  1184.2 61.2 %all-gather.30.cloned.1.call-done = bf16[2048,1408]{1,0:T(8,128)(2,1)} async-done(((bf16[1024,1408]{1,0:T(8,128)(2,1)}), bf16[2048,1408]{1,0:T(8,128)(2,1)}) %all-gather.30.cloned.1.call-update) | async-done | bytes 5767184 | tf_op jit(solution)/shard_map/all_gather | solution.py:232
  1249.8 71.6 %all-gather.28.cloned.1.call-done = bf16[2048,1408]{1,0:T(8,128)(2,1)} async-done(((bf16[1024,1408]{1,0:T(8,128)(2,1)}), bf16[2048,1408]{1,0:T(8,128)(2,1)}) %all-gather.28.cloned.1.call-update) | async-done | bytes 5767184 | tf_op jit(solution)/shard_map/all_gather | solution.py:231
  1325.9 71.6 %all-gather.32.cloned.1.call-done = bf16[1408,2048]{1,0:T(8,128)(2,1)} async-done(((bf16[704,2048]{1,0:T(8,128)(2,1)}), bf16[1408,2048]{1,0:T(8,128)(2,1)}) %all-gather.32.cloned.1.call-update) | async-done | bytes 5767184 | tf_op jit(solution)/shard_map/all_gather | solution.py:233
  1402.5 16.9 all_gather.112
  1419.4 13.0 all_gather.111
  1432.4 13.1 all_gather.113
  1458.2 10.7 gather_fusion.1
  1468.8 6.5 reshape.334
  1475.4 7.3 multiply_reduce_fusion
  1482.8 11.0 gather_fusion.3
  1493.8 6.9 reshape.335
  1500.7 6.0 reduce_sum.205
  1517.2 7.3 convolution_convert_fusion.2
  1560.7 9.6 all_gather.104
  1575.2 6.1 fusion.42
  1582.2 8.0 fusion.58
  1590.2 27.0 %all-gather.40.cloned.1.call-done = bf16[256,4096]{0,1:T(8,128)(2,1)} async-done(((bf16[128,4096]{0,1:T(8,128)(2,1)}), bf16[256,4096]{0,1:T(8,128)(2,1)}) %all-gather.40.cloned.1.call-update) | async-done | bytes 2097168 | tf_op jit(solution)/shard_map/all_gather | solution.py:398
  1624.2 15.0 convolution_bitcast_fusion.2
  1639.3 13.9 convolution_bitcast_fusion
  1653.2 13.1 convolution_bitcast_fusion.1
  1675.3 7.1 all-reduce.7
  1682.5 36.6 %all-reduce.5 = (f32[1024]{0:T(1024)}, f32[256]{0:T(256)}, f32[1024]{0:T(1024)}) all-reduce(f32[1024]{0:T(1024)S(1)} %dynamic-slice.1, f32[256]{0:T(256)S(1)} %dynamic-slice.3, f32[1024]{0:T(1024)S(1)} %dynamic-slice.5), channel_id=1, replica_groups=mesh['expert'=16,'shard'=2] {'expert'}, use_global_device_ids=true, to_apply=%region_26.27 | all-reduce | flops 2304 | bytes 18432 | tf_op jit(solution)/shard_map/psum | solution.py:434
  1726.8 652.1 %all-reduce.10.cloned.1.call-done = (f32[1024,3072]{1,0:T(8,128)}, f32[1024,576]{0,1:T(8,128)}, f32[256,4096]{1,0:T(8,128)}, f32[1024,2048]{1,0:T(8,128)}, f32[1...) async-done(((f32[1024,3072]{1,0:T(8,128)}, f32[1024,576]{0,1:T(8,128)}, f32[256,4096]{1,0:T(8,128)}, f32[1024,2048]{1,0:T(8,128)}, ...) | async-done | bytes 44892176 | tf_op jit(solution)/shard_map/psum | solution.py:434
  2378.9 11.1 copy.144
  2401.3 5.7 copy.149
  (359 shorter events, 189.5 us)
Async XLA Ops:
  7.2 833.3 %copy-start = (bf16[1,704,2048]{2,1,0:T(8,128)(2,1)S(1)}, bf16[1,704,2048]{2,1,0:T(8,128)(2,1)}, u32[]{:S(2)}) copy-start(bf16[1,704,2048]{2,1,0:T(8,128)(2,1)} %param.34) | copy-start | bytes 8650756
  7.2 41.2 %all-gather.18.cloned.1.call-start = ((), (), s32[]{:S(2)}) async-start(), calls=%async_computation.6 | async-start | bytes 3538944 | tf_op jit(solution)/shard_map/all_gather | solution.py:225
  7.9 98.8 %all-gather.20.cloned.1.call-start = ((), (), s32[]{:S(2)}) async-start(), calls=%async_computation.7 | async-start | bytes 6291456 | tf_op jit(solution)/shard_map/all_gather | solution.py:227
  8.7 22.9 copy-start.8
  8.7 252.1 %all-gather.22.cloned.1.call-start = ((), (), s32[]{:S(2)}) async-start(), calls=%async_computation.8 | async-start | bytes 18874368 | tf_op jit(solution)/shard_map/all_gather | solution.py:224
  9.5 356.8 %all-gather.24.cloned.1.call-start = ((), (), s32[]{:S(2)}) async-start(), calls=%async_computation.9 | async-start | bytes 12582912 | tf_op jit(solution)/shard_map/all_gather | solution.py:228
  15.6 95.0 %copy-start.63 = (f32[2,1,256]{2,1,0:T(1,128)}, f32[2,1,256]{2,1,0:T(1,128)S(1)}, u32[]{:S(2)}) copy-start(f32[2,1,256]{2,1,0:T(1,128)S(1)} %convert_element_type.152) | copy-start | bytes 6148
  20.0 31.8 %copy-start.48 = (f32[2048]{0:T(1024)}, f32[2048]{0:T(1024)S(1)}, u32[]{:S(2)}) copy-start(f32[2048]{0:T(1024)S(1)} %convert_element_type.118) | copy-start | bytes 24580
  24.4 346.9 %copy-start.42 = (f32[2048]{0:T(1024)}, f32[2048]{0:T(1024)S(1)}, u32[]{:S(2)}) copy-start(f32[2048]{0:T(1024)S(1)} %convert_element_type.125) | copy-start | bytes 24580
  31.9 19.3 copy-start.70
  33.4 18.4 copy-start.44
  33.4 18.4 copy-start.46
  52.0 217.1 %copy-start.25 = (bf16[128,512]{0,1:T(8,128)(2,1)}, bf16[128,512]{0,1:T(8,128)(2,1)S(1)}, u32[]{:S(2)}) copy-start(bf16[128,512]{0,1:T(8,128)(2,1)S(1)} %multiply_convert_fusion.9) | copy-start | bytes 393220
  271.7 99.5 %copy-start.58 = (f32[16,128]{1,0:T(8,128)}, f32[16,128]{1,0:T(8,128)S(1)}, u32[]{:S(2)}) copy-start(f32[16,128]{1,0:T(8,128)S(1)} %fusion.36) | copy-start | bytes 24580
  381.2 120.0 %all-to-all-start = ((bf16[16,96,2048]{2,1,0:T(8,128)(2,1)}), bf16[16,96,2048]{2,1,0:T(8,128)(2,1)}, u32[]{:S(2)}, u32[]{:S(2)}) async-start(bf16[16,96,2048]{2,1,0:T(8,128)(2,1)} %bitcast.121), calls=%async_computation | async-start | bytes 12582912 | tf_op jit(solution)/shard_map/all_to_all | solution.py:265
  387.0 300.9 %all-gather.26.cloned.1.call-start = ((), (), s32[]{:S(2)}) async-start(), calls=%async_computation.10 | async-start | bytes 18874368 | tf_op jit(solution)/shard_map/all_gather | solution.py:266
  405.3 96.0 %copy-start.53 = (f32[128,6]{0,1:T(8,128)}, f32[128,6]{0,1:T(8,128)S(1)}, u32[]{:S(2)}) copy-start(f32[128,6]{0,1:T(8,128)S(1)} %get-tuple-element.25) | copy-start | bytes 9220
  405.3 96.0 %copy-start.72 = (f32[128]{0:T(128)}, f32[128]{0:T(128)S(1)}, u32[]{:S(2)}) copy-start(f32[128]{0:T(128)S(1)} %get-tuple-element.24) | copy-start | bytes 1540
  501.3 339.2 %all-gather.34.cloned.1.call-start = ((), (), s32[]{:S(2)}) async-start(), calls=%async_computation.15 | async-start | bytes 18874368 | tf_op jit(solution)/shard_map/all_gather | solution.py:312
  687.9 334.2 %reduce-scatter.3.cloned.1.call-start = ((), (), s32[]{:S(2)}) async-start(), calls=%async_computation.11 | async-start | bytes 18874368 | tf_op jit(solution)/shard_map/reduce_scatter | solution.py:276
  688.0 15.8 copy-start.78
  688.0 15.8 copy-start.79
  877.5 291.4 %reduce-scatter.5.cloned.1.call-start = ((), (), s32[]{:S(2)}) async-start(), calls=%async_computation.16 | async-start | bytes 18874368 | tf_op jit(solution)/shard_map/reduce_scatter | solution.py:323
  914.5 330.8 %all-gather.30.cloned.1.call-start = ((), (), s32[]{:S(2)}) async-start(), calls=%async_computation.13 | async-start | bytes 8650752 | tf_op jit(solution)/shard_map/all_gather | solution.py:232
  1022.1 146.8 %all-to-all-start.1 = ((bf16[16,96,2048]{2,1,0:T(8,128)(2,1)}), bf16[16,96,2048]{2,1,0:T(8,128)(2,1)}, u32[]{:S(2)}, u32[]{:S(2)}) async-start(bf16[16,96,2048]{2,1,0:T(8,128)(2,1)} %bitcast.126), calls=%async_computation.2 | async-start | bytes 12582912 | tf_op jit(solution)/shard_map/all_to_all | solution.py:282
  1027.8 293.6 %all-gather.28.cloned.1.call-start = ((), (), s32[]{:S(2)}) async-start(), calls=%async_computation.12 | async-start | bytes 8650752 | tf_op jit(solution)/shard_map/all_gather | solution.py:231
  1028.3 369.1 %all-gather.32.cloned.1.call-start = ((), (), s32[]{:S(2)}) async-start(), calls=%async_computation.14 | async-start | bytes 8650752 | tf_op jit(solution)/shard_map/all_gather | solution.py:233
  1168.9 76.4 %copy-start.5 = (bf16[128,2048]{1,0:T(8,128)(2,1)S(1)}, bf16[128,2048]{1,0:T(8,128)(2,1)}, u32[]{:S(2)}) copy-start(bf16[128,2048]{1,0:T(8,128)(2,1)} %multiply_convert_fusion.4) | copy-start | bytes 1572868
  1168.9 313.9 %all-to-all-start.3 = ((bf16[16,96,2048]{2,1,0:T(8,128)(2,1)}), bf16[16,96,2048]{2,1,0:T(8,128)(2,1)}, u32[]{:S(2)}, u32[]{:S(2)}) async-start(bf16[16,96,2048]{2,1,0:T(8,128)(2,1)} %bitcast.125), calls=%async_computation.5 | async-start | bytes 12582912 | tf_op jit(solution)/shard_map/all_to_all | solution.py:331
  1174.7 270.9 %all-gather.48.cloned.1.call-start = ((), (), s32[]{:S(2)}) async-start(), calls=%async_computation.23 | async-start | bytes 1572864 | tf_op jit(solution)/shard_map/all_gather | solution.py:406
  1175.3 278.3 %all-gather.46.cloned.1.call-start = ((), (), s32[]{:S(2)}) async-start(), calls=%async_computation.22 | async-start | bytes 1572864 | tf_op jit(solution)/shard_map/all_gather | solution.py:401
  1176.0 396.2 %all-gather.36.cloned.1.call-start = ((), (), s32[]{:S(2)}) async-start(), calls=%async_computation.17 | async-start | bytes 1572864 | tf_op jit(solution)/shard_map/all_gather | solution.py:394
  1176.6 398.5 %all-gather.42.cloned.1.call-start = ((), (), s32[]{:S(2)}) async-start(), calls=%async_computation.20 | async-start | bytes 1572864 | tf_op jit(solution)/shard_map/all_gather | solution.py:399
  1184.1 391.1 %all-gather.44.cloned.1.call-start = ((), (), s32[]{:S(2)}) async-start(), calls=%async_computation.21 | async-start | bytes 1572864 | tf_op jit(solution)/shard_map/all_gather | solution.py:400
  1325.9 119.7 %copy-start.57 = (f32[16,128]{1,0:T(8,128)S(1)}, f32[16,128]{1,0:T(8,128)}, u32[]{:S(2)}) copy-start(f32[16,128]{1,0:T(8,128)} %copy-done.56) | copy-start | bytes 24580
  1325.9 119.7 %copy-start.59 = (f32[16,128]{1,0:T(8,128)S(1)}, f32[16,128]{1,0:T(8,128)}, u32[]{:S(2)}) copy-start(f32[16,128]{1,0:T(8,128)} %copy-done.58) | copy-start | bytes 24580
  1402.4 30.0 %copy-start.22 = (bf16[128,1408]{1,0:T(8,128)(2,1)}, bf16[128,1408]{1,0:T(8,128)(2,1)S(1)}, u32[]{:S(2)}) copy-start(bf16[128,1408]{1,0:T(8,128)(2,1)S(1)} %get-tuple-element.47) | copy-start | bytes 1081348
  1402.4 43.1 %copy-start.24 = (bf16[128,1408]{1,0:T(8,128)(2,1)}, bf16[128,1408]{1,0:T(8,128)(2,1)S(1)}, u32[]{:S(2)}) copy-start(bf16[128,1408]{1,0:T(8,128)(2,1)S(1)} %get-tuple-element.46) | copy-start | bytes 1081348
  1529.0 53.2 %all-gather.38.cloned.1.call-start = ((), (), s32[]{:S(2)}) async-start(), calls=%async_computation.18 | async-start | bytes 2359296 | tf_op jit(solution)/shard_map/all_gather | solution.py:395
  1538.0 79.2 %all-gather.40.cloned.1.call-start = ((), (), s32[]{:S(2)}) async-start(), calls=%async_computation.19 | async-start | bytes 3145728 | tf_op jit(solution)/shard_map/all_gather | solution.py:398
  1552.1 826.7 %all-reduce.10.cloned.1.call-start = ((), (), s32[]{:S(2)}) async-start(), calls=%async_computation.24 | async-start | bytes 89784320 | tf_op jit(solution)/shard_map/psum | solution.py:434
  1581.3 36.0 %copy-start.30 = (bf16[256,512]{0,1:T(8,128)(2,1)S(1)}, bf16[256,512]{0,1:T(8,128)(2,1)}, u32[]{:S(2)}) copy-start(bf16[256,512]{0,1:T(8,128)(2,1)} %all_gather.105) | copy-start | bytes 786436
  1621.6 17.6 slice-start.10
  1624.2 29.0 %slice-start.7 = ((s8[12582912]{0:T(1024)(128)(4,1)}), s8[4194304]{0:T(1024)(128)(4,1)S(1)}, s32[]{:S(2)}) async-start(s8[12582912]{0:T(1024)(128)(4,1)} %bitcast.149), calls=%async_computation.32 | async-start | bytes 8388608
  1624.2 29.0 %slice-start.8 = ((s8[12582912]{0:T(1024)(128)(4,1)}), s8[4194304]{0:T(1024)(128)(4,1)S(1)}, s32[]{:S(2)}) async-start(s8[12582912]{0:T(1024)(128)(4,1)} %bitcast.149), calls=%async_computation.33 | async-start | bytes 8388608
  1639.2 27.1 %slice-start = ((s8[12582912]{0:T(1024)(128)(4,1)}), s8[4194304]{0:T(1024)(128)(4,1)S(1)}, s32[]{:S(2)}) async-start(s8[12582912]{0:T(1024)(128)(4,1)} %bitcast.118), calls=%async_computation.25 | async-start | bytes 8388608
  1639.3 27.1 %slice-start.1 = ((s8[12582912]{0:T(1024)(128)(4,1)}), s8[4194304]{0:T(1024)(128)(4,1)S(1)}, s32[]{:S(2)}) async-start(s8[12582912]{0:T(1024)(128)(4,1)} %bitcast.118), calls=%async_computation.26 | async-start | bytes 8388608
  1666.4 52.7 %copy-start.23 = (bf16[128,1408]{1,0:T(8,128)(2,1)S(1)}, bf16[128,1408]{1,0:T(8,128)(2,1)}, u32[]{:S(2)}) copy-start(bf16[128,1408]{1,0:T(8,128)(2,1)} %copy-done.22) | copy-start | bytes 1081348
  (69 other events, 471.1 us)
Sparse Core Ops, SparseCore 0:
  9.6 38.7 all-gather.17
  49.9 56.7 all-gather.19
  108.3 152.5 all-gather.21
  262.2 103.9 all-gather.23
  501.4 174.9 all-gather.25
  688.0 152.3 all-gather.33
  877.6 144.4 reduce-scatter.2
  1024.4 144.4 reduce-scatter.4
  1170.4 74.8 all-gather.29
  1246.7 74.6 all-gather.27
  1322.9 74.4 all-gather.31
  1398.8 30.0 all-gather.47
  1430.5 23.0 all-gather.45
  1455.5 21.3 all-gather.35
  1478.3 21.2 all-gather.41
  1529.2 21.2 all-gather.43
  1551.8 30.3 all-gather.37
  1584.2 33.0 all-gather.39
  1624.1 754.6 all-reduce.9
where the time goes:
time: 2430 us; the launch traced here: 2420 us
  waiting for transfers between devices  1670 us (69%)
  blocking collectives  293 us (12%)
  matrix products  262 us (11%)
  local copies, waits for them, and re-layouts  126 us (5%)
  other arithmetic  33.6 us (1%)
    psum x1, waiting for transfers between devices, body(): lax.psum((shares[0], shares[1], shares[2], shares[3], shares[4], shares[5...  652 us
    all_to_all x1, blocking collectives, body(): lax.all_to_all(send_grads, 'expert', split_axis=0, concat_axis=0, tiled=T...  166 us
    all_gather x1, waiting for transfers between devices, body(): lax.all_gather(w_query, 'shard', axis=0, tiled=True)  146 us
    reduce_scatter x1, waiting for transfers between devices, body(): lax.psum_scatter((trail_product(pre_gate_grad, gate_local) + trail_produc...  140 us
    all_gather x1, waiting for transfers between devices, body(): lax.all_gather(arrived_grads.reshape(owners * capacity, model_width), 'sh...  125 us
    reduce_scatter x1, waiting for transfers between devices, body(): lax.psum_scatter(plain_product(hidden, down_local).astype(jnp.bfloat16),...  107 us
    all_to_all x1, waiting for transfers between devices, body(): lax.all_to_all(send_rows, 'expert', split_axis=0, concat_axis=0, tiled=True)  95.9 us
    all_gather x1, waiting for transfers between devices, body(): lax.all_gather(w_output, 'shard', axis=0, tiled=True)  93.4 us
  transfers between devices with their start and end apart: 22, of which 15 were waited for; matrix products, arithmetic and copies ran while one was open for 14% of the time, Pallas kernels for 0%

commit v1 on v0

v1 whole, which is shorter than its diff:
```python
import functools

import jax
import jax.numpy as jnp
import numpy as np
from jax import lax
from jax.experimental import pallas as pl
from jax.experimental.pallas import tpu as pltpu
from jax.sharding import PartitionSpec as P

HEADS = 16
NOPE = 128
ROPE = 64
VDIM = 128
KVR = 512
NORM_EPSILON = 1e-06
ROTARY_BASE = 50000.0
ROUTE_SCALE = 2.446
NEGATIVE = -1e30
F32 = jnp.float32
BF16 = jnp.bfloat16


def dot(a, b):
    return jnp.dot(a, b, preferred_element_type=F32)


def dot_tl(a, b):
    return lax.dot_general(a, b, (((0,), (0,)), ((), ())), preferred_element_type=F32)


def dot_tr(a, b):
    return lax.dot_general(a, b, (((1,), (1,)), ((), ())), preferred_element_type=F32)


def norm_scale(values):
    return lax.rsqrt(jnp.mean(values * values, axis=-1, keepdims=True) + NORM_EPSILON)


def zero_of(*marks):
    total = jnp.zeros((), F32)
    for mark in jax.tree.leaves(marks):
        one = lax.slice(mark, (0,) * mark.ndim, (1,) * mark.ndim).reshape(())
        total = total + (one != one).astype(F32)
    return total


def after(value, *marks):
    zero = zero_of(*marks)
    return jax.tree.map(lambda v: v + zero.astype(v.dtype), value)


def add_b(a, b):
    return (a.astype(F32) + b.astype(F32)).astype(BF16)


class Net:
    def __init__(self):
        self.E = lax.axis_size("expert")
        self.S = lax.axis_size("shard")
        nx = self.S if self.E % (2 * self.S) == 0 else 1
        nc = 2 if self.E % 2 == 0 else 1
        self.n = {"c": nc, "x": nx, "z": self.E // (nc * nx), "y": self.S}
        self.stride = {"c": 1, "x": nc, "z": nc * nx}
        self.e = lax.axis_index("expert")
        self.s = lax.axis_index("shard")

    def pos(self, axis):
        if axis == "y":
            return self.s
        return (self.e // self.stride[axis]) % self.n[axis]

    def hop(self, value, axis, k=1):
        n = self.n[axis]
        if axis == "y":
            return lax.ppermute(value, "shard", [(i, (i + k) % n) for i in range(n)])
        st = self.stride[axis]
        pairs = []
        for i in range(self.E):
            p = (i // st) % n
            pairs.append((i, i + ((p + k) % n - p) * st))
        return lax.ppermute(value, "expert", pairs)

    def ring_gather(self, value, axis):
        n = self.n[axis]
        out = [None] * n
        out[0] = value
        cur = value
        for k in range(1, n):
            cur = self.hop(cur, axis)
            out[n - k] = cur
        return out

    def ring_scatter(self, value, axis, dim, add):
        n = self.n[axis]
        take = lambda r: lax.index_in_dim(value, r, dim, keepdims=False)
        acc = take(n - 1)
        for k in range(1, n):
            acc = add(take(n - 1 - k), self.hop(acc, axis))
        return acc

    def absolute(self, pieces, axis, dim):
        n = self.n[axis]
        i = self.pos(axis)
        if n == 1:
            return pieces[0]
        if n == 2:
            first = jnp.concatenate(pieces, axis=dim)
            second = jnp.concatenate(pieces[::-1], axis=dim)
            return jnp.where(i == 0, first, second)
        size = pieces[0].shape[dim]
        twice = jnp.concatenate(list(pieces) * 2, axis=dim)
        return lax.dynamic_slice_in_dim(twice, ((n - i) % n) * size, n * size, dim)

    def gather_part(self, value, mid, mark):
        last = "y" if mid == "x" else "x"
        cur = jnp.stack(self.ring_gather(value, "z"), axis=0)
        pieces = self.ring_gather(cur, mid)
        cur = jnp.stack(pieces[:1] + after(pieces[1:], mark), axis=0)
        return self.ring_gather(cur, "c"), self.ring_gather(cur, last)[1:]

    def scatter_cores(self, bufs):
        return [self.ring_list(pieces, "c") for pieces in bufs]

    def scatter_stage(self, lists, axes, work=None):
        n = max(self.n[axis] for axis in axes)
        accs = [pieces[self.n[axis] - 1] for pieces, axis in zip(lists, axes)]
        for k in range(1, n):
            got = [
                self.hop(acc, axis) if k < self.n[axis] else None for acc, axis in zip(accs, axes)
            ]
            job = None
            if work:
                job = work.pop(0)
            if job is not None:
                mark = job(accs)
                got = [g if g is None else after(g, mark) for g in got]
            accs = [
                acc if g is None else add_b(pieces[self.n[axis] - 1 - k], g)
                for acc, g, pieces, axis in zip(accs, got, lists, axes)
            ]
        return accs

    def scatter_both(self, sums_1, sums_2, work=None):
        work = list(work or [])
        split = lambda v: [v[k] for k in range(v.shape[0])]
        one, two = self.scatter_stage([sums_1, sums_2], ("y", "x"), work)
        one, two = self.scatter_stage([split(one), split(two)], ("x", "y"), work)
        rows = [jnp.concatenate([one[k], two[k]], axis=0) for k in range(self.n["z"])]
        return self.scatter_stage([rows], ("z",), work)[0]

    def ring_list(self, pieces, axis):
        n = self.n[axis]
        acc = pieces[n - 1]
        for k in range(1, n):
            acc = add_b(pieces[n - 1 - k], self.hop(acc, axis))
        return acc

    def reduce_steps(self, value, order):
        for axis in order:
            n, i = self.n[axis], self.pos(axis)
            if n == 1:
                continue
            rows = value.shape[0] // n
            take = lambda k, v=value: lax.dynamic_slice_in_dim(v, (k % n) * rows, rows, 0)
            got = yield [(take(i + k), axis, k) for k in range(1, n)]
            total = take(i).astype(F32)
            for piece in got:
                total = total + piece.astype(F32)
            value = total.astype(BF16)
        return value

    def spread_steps(self, value, order, dim=0):
        for axis in order[::-1]:
            n = self.n[axis]
            if n == 1:
                continue
            got = yield [(value, axis, k) for k in range(1, n)]
            value = self.absolute([value] + list(got)[::-1], axis, dim)
        return value

    def total_steps(self, value, order):
        value = yield from self.reduce_steps(value, order)
        value = yield from self.spread_steps(value, order)
        return value

    def in_rounds(self, runs):
        results = [None] * len(runs)
        sends = {k: next(run) for k, run in enumerate(runs)}
        while sends:
            keys = [k for k in sends if sends[k]]
            values = [[v[0] for v in sends[k]] for k in keys]
            got = {
                k: [self.hop(v, item[1], item[2]) for v, item in zip(vs, sends[k])]
                for k, vs in zip(keys, values)
            }
            following = {}
            for k in sends:
                try:
                    following[k] = runs[k].send(got.get(k))
                except StopIteration as stop:
                    results[k] = stop.value
            sends = following
        return results


MEGA = 2**20
LANES = 128


def dot_nt(a, b):
    return lax.dot_general(a, b, (((1,), (1,)), ((), ())), preferred_element_type=F32)


def fill_back(entries):
    out = list(entries)
    for i in reversed(range(len(out) - 1)):
        if out[i] is None:
            out[i] = out[i + 1]
    last = None
    for i in range(len(out)):
        last = out[i] if out[i] is not None else last
        out[i] = last
    return out


def fill_weights(pairs):
    @pl.when(pl.program_id(0) == 0)
    def _():
        for main, extra, held in pairs:
            a, b = main.shape[0], extra.shape[0]
            held[:a, :] = main[...]
            held[a : a + b, :] = extra[...]
            if held.shape[0] > a + b:
                held[a + b :, :] = jnp.zeros((held.shape[0] - a - b, held.shape[1]), BF16)


def padded(main, extra):
    rows = main.shape[0] + extra.shape[0]
    return rows + -rows % 256


def down_kernel(nz, th, width, tab, *refs):
    ins = refs[:nz]
    main_ref, extra_ref, rows_ref, prod_ref, mask_ref, down_ref = refs[nz:]
    fill_weights([(main_ref, extra_ref, down_ref)])
    for z in range(nz):
        rows_ref[0, z * th : (z + 1) * th, :] = ins[z][0, 0, :, :width]
        mask_ref[0, z * th : (z + 1) * th, :] = ins[z][0, 0, :, width:]
    prod_ref[0] = dot_nt(rows_ref[0], down_ref[...])


def down_call(gathered, table, down, th, width):
    nz, count = table.shape[0] // 2, table.shape[1]
    rows = nz * th
    full_width = gathered.shape[-1]
    hid = padded(*down)

    def spec(z):
        return pl.BlockSpec(
            (1, 1, th, full_width), lambda i, tab: (tab[z, i], tab[nz + z, i], 0, 0)
        )

    step = lambda w: pl.BlockSpec((1, rows, w), lambda i, tab: (i, 0, 0))
    whole = lambda a: pl.BlockSpec(a.shape, lambda i, tab: (0, 0), pipeline_mode=pl.Buffered(1))
    return pl.pallas_call(
        functools.partial(down_kernel, nz, th, width),
        grid_spec=pltpu.PrefetchScalarGridSpec(
            num_scalar_prefetch=1,
            grid=(count,),
            in_specs=[spec(z) for z in range(nz)]
            + [whole(a) for a in down],
            out_specs=[step(width), step(hid), step(LANES)],
            scratch_shapes=[pltpu.VMEM((hid, width), BF16)],
        ),
        out_shape=[
            jax.ShapeDtypeStruct((count, rows, width), BF16),
            jax.ShapeDtypeStruct((count, rows, hid), F32),
            jax.ShapeDtypeStruct((count, rows, LANES), BF16),
        ],
        compiler_params=pltpu.CompilerParams(vmem_limit_bytes=48 * MEGA),
        cost_estimate=pl.CostEstimate(
            flops=2 * count * rows * hid * width,
            bytes_accessed=count * rows * (4 * width + 4 * hid) + 2 * hid * width,
            transcendentals=0,
        ),
        name="down_rows",
    )(table, *([gathered] * nz), *down)


def chain_kernel(arrays, th, nz, routed, tile, tab, *refs):
    ins = refs[:arrays]
    prod_ref, mask_ref, gate_a, gate_b, up_a, up_b, router_ref = refs[arrays : arrays + 7]
    outs = refs[arrays + 7 : 2 * arrays + 7]
    rows_ref, pg_ref, pu_ref, gh_ref, held, gate_ref, up_ref = refs[2 * arrays + 7 :]
    fill_weights([(gate_a, gate_b, gate_ref), (up_a, up_b, up_ref)])
    i = pl.program_id(0)
    for k in range(arrays):

        @pl.when(tab[arrays, i] == k)
        def _(k=k):
            for z in range(nz):
                rows_ref[0, z * th : (z + 1) * th, :] = ins[k][0, z]

    x = rows_ref[0]
    width = x.shape[1]
    hid = gate_ref.shape[0]
    own = tab[arrays + 1, 0]
    scores = jax.nn.sigmoid(jnp.dot(x, router_ref[...], preferred_element_type=F32))
    chosen = scores * mask_ref[0].astype(F32)
    lane = lax.broadcasted_iota(jnp.int32, chosen.shape, 1)
    mine = jnp.sum(jnp.where(lane == own, chosen, 0.0), axis=1, keepdims=True)
    gate = ROUTE_SCALE * mine / jnp.sum(chosen, axis=1, keepdims=True)
    on = jnp.sum(
        jnp.where(lane == own, mask_ref[0].astype(F32), 0.0), axis=1, keepdims=True
    )
    gate_grad = None
    for j in range(0, hid, tile):
        sl = slice(j, j + tile)
        pre_gate = dot_nt(x, gate_ref[sl, :])
        pre_up = dot_nt(x, up_ref[sl, :])
        prod = prod_ref[0, :, sl]
        sig = jax.nn.sigmoid(pre_gate)
        act = pre_gate * sig
        hidden = act * pre_up
        scale = gate
        part = hidden * prod
        if j + tile > routed:
            column = j + lax.broadcasted_iota(jnp.int32, part.shape, 1)
            scale = jnp.where(column < routed, gate, 1.0)
            part = jnp.where(column < routed, part, 0.0)
        part = jnp.sum(part, axis=1, keepdims=True)
        gate_grad = part if gate_grad is None else gate_grad + part
        upstream = prod * scale
        pg_ref[0, :, sl] = (upstream * pre_up * (sig + act * (1.0 - sig))).astype(BF16)
        pu_ref[0, :, sl] = (upstream * act).astype(BF16)
        gh_ref[0, :, sl] = (hidden * scale).astype(BF16)
    grad = jnp.dot(pg_ref[0], gate_ref[...], preferred_element_type=F32) + jnp.dot(
        pu_ref[0], up_ref[...], preferred_element_type=F32
    )
    held[:, :width] = grad.astype(BF16)
    held[:, width:] = jnp.where(lane == own, gate_grad * on, 0.0).astype(BF16)
    for k in range(arrays):

        @pl.when(tab[arrays, i] == k)
        def _(k=k):
            for z in range(nz):
                outs[k][0, z] = held[z * th : (z + 1) * th, :]


def chain_call(bufs, first, prod, mask, gate, up, router_pad, own, routed, tie):
    arrays = len(bufs)
    steps = [(k, a) for k, buf in enumerate(bufs) for a in range(buf.shape[0])]
    count = len(steps)
    nz, th, width = bufs[0].shape[1:]
    rows = nz * th
    hid = padded(*gate)
    table = np.zeros((arrays + 1, count), np.int32)
    for j in range(arrays):
        table[j] = fill_back([a if k == j else None for k, a in steps])
    table[arrays] = [k for k, _ in steps]
    tab = jnp.concatenate(
        [jnp.asarray(table), jnp.full((1, count), 1, jnp.int32) * own.astype(jnp.int32)], axis=0
    )
    tab = after(tab, tie)
    wide = width + LANES

    def block(j, w):
        return pl.BlockSpec((1, nz, th, w), lambda i, tab: (tab[j, i], 0, 0, 0))

    step = lambda w, base=0: pl.BlockSpec((1, rows, w), lambda i, tab: (i + base, 0, 0))
    whole = lambda a: pl.BlockSpec(a.shape, lambda i, tab: (0, 0), pipeline_mode=pl.Buffered(1))
    return pl.pallas_call(
        functools.partial(chain_kernel, arrays, th, nz, routed, 256),
        grid_spec=pltpu.PrefetchScalarGridSpec(
            num_scalar_prefetch=1,
            grid=(count,),
            in_specs=[block(j, width) for j in range(arrays)]
            + [step(hid, first), step(LANES, first)]
            + [whole(a) for a in (*gate, *up, router_pad)],
            out_specs=[block(j, wide) for j in range(arrays)]
            + [step(width), step(hid), step(hid), step(hid)],
            scratch_shapes=[pltpu.VMEM((rows, wide), BF16)]
            + [pltpu.VMEM((hid, width), BF16)] * 2,
        ),
        out_shape=[jax.ShapeDtypeStruct((*buf.shape[:3], wide), BF16) for buf in bufs]
        + [jax.ShapeDtypeStruct((count, rows, width), BF16)]
        + [jax.ShapeDtypeStruct((count, rows, hid), BF16)] * 3,
        compiler_params=pltpu.CompilerParams(vmem_limit_bytes=56 * MEGA),
        cost_estimate=pl.CostEstimate(
            flops=8 * count * rows * hid * width,
            bytes_accessed=count * rows * (6 * width + 10 * hid) + 4 * hid * width,
            transcendentals=count * rows * hid,
        ),
        name="expert_chain",
    )(tab, *bufs, prod, mask, *gate, *up, router_pad)


def out_kernel(arrays, th, nz, tab, gh_ref, main_ref, extra_ref, *refs):
    outs, held, down_ref = refs[:arrays], refs[arrays], refs[arrays + 1]
    fill_weights([(main_ref, extra_ref, down_ref)])
    i = pl.program_id(0)
    held[...] = jnp.dot(gh_ref[0], down_ref[...], preferred_element_type=F32).astype(BF16)
    for k in range(arrays):

        @pl.when(tab[arrays, i] == k)
        def _(k=k):
            for z in range(nz):
                outs[k][0, z] = held[z * th : (z + 1) * th, :]


def out_call(gated, down, shapes, tie):
    arrays = len(shapes)
    steps = [(k, a) for k, shape in enumerate(shapes) for a in range(shape[0])]
    count = len(steps)
    _, nz, th, width = shapes[0]
    rows = nz * th
    hid = padded(*down)
    table = np.zeros((arrays + 1, count), np.int32)
    for j in range(arrays):
        table[j] = fill_back([a if k == j else None for k, a in steps])
    table[arrays] = [k for k, _ in steps]

    def block(j):
        return pl.BlockSpec((1, nz, th, width), lambda i, tab: (tab[j, i], 0, 0, 0))

    return pl.pallas_call(
        functools.partial(out_kernel, arrays, th, nz),
        grid_spec=pltpu.PrefetchScalarGridSpec(
            num_scalar_prefetch=1,
            grid=(count,),
            in_specs=[
                pl.BlockSpec((1, rows, hid), lambda i, tab: (i, 0, 0)),
            ]
            + [
                pl.BlockSpec(a.shape, lambda i, tab: (0, 0), pipeline_mode=pl.Buffered(1))
                for a in down
            ],
            out_specs=[block(j) for j in range(arrays)],
            scratch_shapes=[pltpu.VMEM((rows, width), BF16), pltpu.VMEM((hid, width), BF16)],
        ),
        out_shape=[jax.ShapeDtypeStruct(shape, BF16) for shape in shapes],
        compiler_params=pltpu.CompilerParams(vmem_limit_bytes=48 * MEGA),
        cost_estimate=pl.CostEstimate(
            flops=2 * count * rows * hid * width,
            bytes_accessed=count * rows * 2 * (width + hid) + 2 * hid * width,
            transcendentals=0,
        ),
        name="expert_out",
    )(after(jnp.asarray(table), tie), gated, *down)


def weight_kernel(calls, per, outs_n, hid, extra, tie_ref, *refs):
    lefts, rights = refs[: calls * outs_n], refs[calls * outs_n : calls * (outs_n + 1)]
    outs = refs[calls * (outs_n + 1) :]
    i = pl.program_id(0)

    @pl.when(i == 0)
    def _():
        for o in outs:
            o[...] = jnp.zeros_like(o)

    for c in range(calls):

        @pl.when(i // per == c)
        def _(c=c):
            right = rights[c][0]
            for k in range(outs_n):
                full = lax.dot_general(
                    lefts[k * calls + c][0],
                    right,
                    (((0,), (0,)), ((), ())),
                    preferred_element_type=F32,
                )
                outs[k][...] += full[:hid]
                outs[outs_n + k][...] += full[hid : hid + extra]


def weight_call(lefts, rights, hid, extra, tie):
    calls, outs_n = len(rights), len(lefts)
    bases = [r[1] if len(r) > 1 else 0 for r in rights]
    rights = [r[0] for r in rights]
    per, rows, pad = lefts[0][0].shape
    width = rights[0].shape[2]
    if per % 2 == 0 and rows <= 256:
        rights = [r.reshape(r.shape[0] // 2, 2 * rows, width) for r in rights]
        lefts = [[a.reshape(per // 2, 2 * rows, pad) for a in left] for left in lefts]
        per, rows, bases = per // 2, 2 * rows, [base // 2 for base in bases]

    def spec(c, w, base=0):
        return pl.BlockSpec(
            (1, rows, w), lambda i: (base + jnp.clip(i - c * per, 0, per - 1), 0, 0)
        )

    return pl.pallas_call(
        functools.partial(weight_kernel, calls, per, outs_n, hid, extra),
        grid=(calls * per,),
        in_specs=[pl.BlockSpec(memory_space=pl.ANY)]
        + [spec(c, pad) for _ in range(outs_n) for c in range(calls)]
        + [spec(c, width, bases[c]) for c in range(calls)],
        out_specs=[pl.BlockSpec((hid, width), lambda i: (0, 0))] * outs_n
        + [pl.BlockSpec((extra, width), lambda i: (0, 0))] * outs_n,
        out_shape=[jax.ShapeDtypeStruct((hid, width), F32)] * outs_n
        + [jax.ShapeDtypeStruct((extra, width), F32)] * outs_n,
        compiler_params=pltpu.CompilerParams(vmem_limit_bytes=58 * MEGA),
        cost_estimate=pl.CostEstimate(
            flops=2 * outs_n * calls * per * rows * pad * width,
            bytes_accessed=calls * per * rows * 2 * (outs_n * pad + width) + 4 * outs_n * hid * width,
            transcendentals=0,
        ),
        name="expert_weights",
    )(after(jnp.zeros((8, LANES), F32), tie), *[a for left in lefts for a in left], *rights)


def rotary_tables(segment_row):
    length = segment_row.shape[-1]
    places = jnp.arange(length, dtype=jnp.int32)
    same_document = segment_row[:, :, None] == segment_row[:, None, :]
    position = jnp.sum(
        jnp.where(same_document & (places[None, :] < places[:, None])[None], 1.0, 0.0), axis=2
    )
    half_rope = ROPE // 2
    frequency = ROTARY_BASE ** (-2.0 * jnp.arange(half_rope, dtype=F32) / ROPE)
    angles = position[:, :, None] * frequency
    cosine = jnp.concatenate([jnp.cos(angles), jnp.cos(angles)], axis=-1)
    sine_table = jnp.concatenate([jnp.sin(angles), jnp.sin(angles)], axis=-1)
    allowed = same_document & (places[None, :] <= places[:, None])[None]
    return cosine, sine_table, allowed


def rotate(values, cosine, sine_table):
    half_rope = values.shape[-1] // 2
    turned = jnp.concatenate([-values[..., half_rope:], values[..., :half_rope]], axis=-1)
    return values * cosine + turned * sine_table


def unrotate(upstream, cosine, sine_table):
    half_rope = upstream.shape[-1] // 2
    weighted = upstream * sine_table
    turned = jnp.concatenate([weighted[..., half_rope:], -weighted[..., :half_rope]], axis=-1)
    return upstream * cosine + turned


def einsum(pattern, a, b):
    return jnp.einsum(pattern, a, b, preferred_element_type=F32)


def body(
    tokens,
    segment_ids,
    routes,
    attn_gain,
    w_query,
    w_latent,
    latent_gain,
    w_keyval,
    w_output,
    ffn_gain,
    w_router,
    shared_gate,
    shared_up,
    shared_down,
    expert_gate,
    expert_up,
    expert_down,
    cotangent,
):
    net = Net()
    S, E, s, e = net.S, net.E, net.s, net.e
    T, D = tokens.shape
    DK = D // S
    HL = HEADS // S
    HQ = HL * (NOPE + ROPE)
    HV = HL * (NOPE + VDIM)
    HID = shared_down.shape[0]
    blocks = list(range(S))

    def cols(value, index, size):
        return lax.dynamic_slice_in_dim(value, (index % S) * size, size, value.ndim - 1)

    def pair_rows(value):
        return jnp.stack(net.ring_gather(value, "y"), axis=0)

    def pair_sum_blocks(parts):
        total = parts[0].astype(F32)
        for r in range(1, S):
            total = total + net.hop(parts[r].astype(BF16), "y", r).astype(F32)
        return total

    KR = KVR // S
    packed = jnp.concatenate(
        [
            w_router.T,
            ffn_gain[None],
            jnp.pad(latent_gain, (0, DK - KR))[None],
        ],
        axis=0,
    )
    packed = net.ring_gather(packed, "y")
    router_full = net.absolute([p[:E] for p in packed], "y", 1)
    ffn_gain_full = net.absolute([p[E] for p in packed], "y", 0).astype(F32)
    latent_gain_full = net.absolute([p[E + 1, :KR] for p in packed], "y", 0).astype(F32)
    inputs = tokens.astype(F32)
    scale_one = norm_scale(inputs)
    rows2 = jnp.concatenate([segment_ids.astype(F32), scale_one.reshape(1, T)], axis=0)
    rows2 = jnp.stack(net.ring_gather(rows2, "y"), axis=0)
    seg_pair = rows2[:, 0]
    scales = rows2[:, 1].reshape(S, T, 1)
    x_pieces = [cols(tokens, s, DK)] + [None] * (S - 1)
    for r in range(1, S):
        x_pieces[S - r] = net.hop(cols(tokens, s + r, DK), "y", r)
    x_cols = jnp.stack(x_pieces, axis=0).astype(F32)
    attn_gain_f = attn_gain.astype(F32)
    plain_one = x_cols * scales
    normed_one = (plain_one * attn_gain_f).astype(BF16).reshape(S * T, DK)
    cosine, sine_table, allowed = rotary_tables(seg_pair)

    query_parts = [
        dot(normed_one, cols(w_query, s + r, HQ)).astype(BF16).reshape(S, T, HQ)
        for r in range(1, S)
    ]
    latent_part_own = dot(normed_one, w_latent).reshape(S, T, -1)
    latent_sent = latent_part_own.astype(BF16)
    first = (query_parts, latent_sent)
    query_got = [net.hop(part, "y", r) for r, part in enumerate(query_parts, 1)]
    latent_got = [net.hop(latent_sent, "y", r) for r in range(1, S)]
    core = net.pos("c")
    half_rows = KR // net.n["c"]
    kv_half = lax.dynamic_slice_in_dim(w_keyval, core * half_rows, half_rows, 0)
    kv_pieces = [cols(w_keyval, s, HV)] + [None] * (S - 1)
    for r in range(1, S):
        got = net.hop(after(cols(kv_half, s + r, HV), first), "y", r)
        kv_pieces[S - r] = net.absolute(net.ring_gather(got, "c"), "c", 0)
    keyval_full = net.absolute(kv_pieces, "y", 0)

    HS = HID // E
    HP = -(-HS // 16) * 16
    sh_pieces = [None] * S
    for r in range(S):
        mine = [
            lax.dynamic_slice_in_dim(w, ((s + r) % S) * HID + e * HS, HS, 1).T
            for w in (shared_gate, shared_up)
        ]
        mine = jnp.pad(jnp.stack(mine, axis=0), ((0, 0), (0, HP - HS), (0, 0)))
        mine = after(mine, first)
        sh_pieces[(S - r) % S] = net.hop(mine, "y", r) if r else mine
    sh_slices = net.absolute(sh_pieces, "y", 2)
    sh_down = lax.dynamic_slice_in_dim(shared_down, e * HS, HS, 0)
    sh_down = after(jnp.pad(sh_down, ((0, HP - HS), (0, 0))), first)
    down_t = (expert_down[0], sh_down)
    gate_t = (expert_gate[0].T, sh_slices[0])
    up_t = (expert_up[0].T, sh_slices[1])
    router_pad = jnp.pad(router_full.T, ((0, 0), (0, LANES - E)))

    queries = dot(normed_one, cols(w_query, s, HQ)).reshape(S, T, HQ)
    queries = after(queries, sh_down, sh_slices, keyval_full)
    for r, got in enumerate(query_got, 1):
        queries = queries + jnp.concatenate([got[r:], got[:r]], axis=0).astype(F32)
    queries = queries.reshape(S, T, HL, NOPE + ROPE)

    def block_all_sum(value):
        total = value
        for r in range(1, S):
            got = net.hop(value.astype(BF16), "y", r).astype(F32)
            total = total + jnp.concatenate([got[r:], got[:r]], axis=0)
        return total

    latent_all = latent_part_own
    for r, got in enumerate(latent_got, 1):
        latent_all = latent_all + jnp.concatenate([got[r:], got[:r]], axis=0).astype(F32)
    query_turn = rotate(queries[..., NOPE:], cosine[:, :, None, :], sine_table[:, :, None, :])
    query_b = jnp.concatenate([queries[..., :NOPE], query_turn], axis=-1).astype(BF16)
    latent = latent_all[..., :KVR]
    key_rope = rotate(latent_all[..., KVR:], cosine, sine_table)
    scale_latent = norm_scale(latent)
    latent_normed = (latent * scale_latent * latent_gain_full).astype(BF16)
    keyval = dot(latent_normed.reshape(S * T, KVR), keyval_full).reshape(S, T, HL, NOPE + VDIM)
    key_shared = jnp.broadcast_to(key_rope[:, :, None, :], (S, T, HL, ROPE))
    key_b = jnp.concatenate([keyval[..., :NOPE], key_shared], axis=-1).astype(BF16)
    value_b = keyval[..., NOPE:].astype(BF16)
    att_scale = (NOPE + ROPE) ** (-0.5)
    scores = einsum("bthd,bshd->bhts", query_b, key_b) * att_scale
    scores = jnp.where(allowed[:, None], scores, NEGATIVE)
    peak = jnp.max(scores, axis=-1, keepdims=True)
    raised = jnp.exp(scores - peak)
    probs = raised / jnp.sum(raised, axis=-1, keepdims=True)
    probs_b = probs.astype(BF16)
    attended = einsum("bhts,bshd->bthd", probs_b, value_b).astype(BF16).reshape(S * T, HL * VDIM)
    out_parts = dot(attended, w_output).reshape(S, T, D)
    residual = inputs + pair_sum_blocks([out_parts[r] for r in blocks])
    scale_two = norm_scale(residual)
    normed_two = (residual * scale_two * ffn_gain_full).astype(BF16)

    th = T // 2
    nx, ny, nz, nc = net.n["x"], net.n["y"], net.n["z"], net.n["c"]
    ids = jnp.arange(E, dtype=jnp.int32)
    mask_own = jnp.sum((routes[:, :, None] == ids[None, None, :]).astype(F32), axis=1)
    mask_lanes = jnp.pad(mask_own.astype(BF16), ((0, 0), (0, LANES - E)))
    cot_wide = jnp.concatenate([cotangent, mask_lanes], axis=1)
    cot_gathered = lax.all_gather(cot_wide, ("expert", "shard"), axis=0).reshape(
        E * S, 2, th, D + LANES
    )
    nr = max(nx, ny)
    steps = []
    for r in range(nr):
        for p in range(2):
            for c in range(nc):
                for k in range(nx if p == 0 else ny):
                    steps.append((k, c, r, p) if p == 0 else (r, c, k, p))
    at = {axis: net.pos(axis) for axis in "cxzy"}
    ahead = lambda axis, k: (at[axis] + jnp.asarray(k, jnp.int32)) % net.n[axis]
    step_x, step_c, step_y, step_p = [np.array(v, np.int32) for v in zip(*steps)]
    table = []
    for z in range(nz):
        expert_of = (
            ahead("z", z) * net.stride["z"]
            + ahead("x", step_x) * net.stride["x"]
            + ahead("c", step_c) * net.stride["c"]
        )
        table.append(expert_of * S + ahead("y", step_y))
    table = jnp.stack(table + [jnp.asarray(step_p)] * nz, axis=0).astype(jnp.int32)
    cot_rows, cot_prod, mask_rows = down_call(cot_gathered, table, down_t, th, D)
    tok_1 = net.gather_part(normed_two[:th], "x", mask_rows)
    tok_2 = net.gather_part(normed_two[th:], "y", mask_rows)
    per = len(steps) // nr
    in_1, in_2 = [], []
    x_rows, pg_rows, pu_rows, gh_rows = [], [], [], []
    for r in range(nr):
        if r == 0:
            bufs, tie = tok_1[0] + tok_2[0], ()
        else:
            tie = gh_rows[-1]
            far = after((tok_1[1][r - 1], tok_2[1][r - 1]), tie)
            bufs = net.ring_gather(far[0], "c") + net.ring_gather(far[1], "c")
        got = chain_call(
            bufs, r * per, cot_prod, mask_rows, gate_t, up_t, router_pad, e, HID, tie
        )
        in_1.append(got[:nc])
        in_2.append(got[nc : 2 * nc])
        x_rows.append(got[2 * nc])
        pg_rows.append(got[2 * nc + 1])
        pu_rows.append(got[2 * nc + 2])
        gh_rows.append(got[2 * nc + 3])
    in_sum_1, in_sum_2 = net.scatter_cores(in_1), net.scatter_cores(in_2)
    shapes = [buf.shape for buf in tok_1[0] + tok_2[0]]
    weight_grads, out_sums, out_bufs = {}, [], []

    def weights_of(name, rows, rights, tie):
        weight_grads[name] = weight_call([rows], rights, HID, HS, tie)
        return weight_grads[name]

    def gate_up_work(marks):
        rights = [[v] for v in x_rows]
        one = weights_of("gate", pg_rows, rights, marks)
        return [weights_of("up", pu_rows, rights, one[1])[1]]

    def down_work(marks):
        rights = [(cot_rows, r * per) for r in range(nr)]
        return weights_of("down", gh_rows, rights, marks)[1]

    def out_work(r):
        def job(marks):
            out_bufs.append(out_call(gh_rows[r], down_t, shapes, marks))
            return out_bufs[-1][0]

        return job

    def out_sum_work(marks):
        for bufs in out_bufs:
            out_sums.append([net.ring_list(bufs[:nc], "c"), net.ring_list(bufs[nc:], "c")])
        return [v[0] for v in out_sums]

    hops = max(nx, ny) - 1
    work = [gate_up_work] + [None] * (hops - 1) + [down_work] + [None] * (hops - 1)
    early = min(nr, nz - 2)
    work += [out_work(r) for r in range(early)]
    if early == nr:
        work.append(out_sum_work)
    in_wide = net.scatter_both(in_sum_1, in_sum_2, work)
    gate_w_grad, sh_gate_rows = weight_grads["gate"]
    up_w_grad, sh_up_rows = weight_grads["up"]
    down_grad, sh_down_rows = weight_grads["down"]
    in_grad = in_wide[:, :D]
    gate_grads_raw = in_wide[:, D : D + E].astype(F32)

    def gather_cols(value, width):
        pieces = [value.reshape(S, T, width)] + [None] * (S - 1)
        for r in range(1, S):
            got = net.hop(value.reshape(S, T, width), "y", r)
            pieces[S - r] = jnp.concatenate([got[r:], got[:r]], axis=0)
        return net.absolute(pieces, "y", 2).reshape(S * T, S * width)

    def own_cols(value):
        pieces = [value[0].astype(BF16)] + [None] * (S - 1)
        for r in range(1, S):
            pieces[S - r] = net.hop(value[r].astype(BF16), "y", r)
        return net.absolute(pieces, "y", 1).astype(F32)

    scores_own = jax.nn.sigmoid(dot_tr(normed_two, router_full))
    gate_grads = gate_grads_raw * mask_own
    picked = scores_own * mask_own
    picked_total = jnp.sum(picked, axis=1, keepdims=True)
    weighted = jnp.sum(gate_grads * picked, axis=1, keepdims=True)
    picked_grad = ROUTE_SCALE * (
        gate_grads / picked_total - weighted / (picked_total * picked_total)
    )
    logit_grad_b = (picked_grad * picked * (1.0 - picked)).astype(BF16)
    normed_two_grad = in_grad.astype(F32) + dot(logit_grad_b, router_full)
    upstream = cotangent.astype(F32)
    plain_two = residual * scale_two
    ffn_gain_part = jnp.sum(normed_two_grad * plain_two, axis=0)
    inner = normed_two_grad * ffn_gain_full
    residual_grad = upstream + scale_two * (
        inner - plain_two * jnp.mean(inner * plain_two, axis=-1, keepdims=True)
    )
    router_grad_part = dot_tl(normed_two, logit_grad_b)

    room = ((0, HP - HS), (0, 0))
    sh_gu = jnp.stack([jnp.pad(v.astype(BF16), room) for v in (sh_gate_rows, sh_up_rows)], axis=0)
    sh_down_own = jnp.pad(sh_down_rows.astype(BF16), room)
    gu_pieces = [None] * S
    for r in range(S):
        piece = cols(sh_gu, s + r, DK)
        gu_pieces[(S - r) % S] = net.hop(piece, "y", r) if r else piece
    gu_own = net.absolute([piece[:, None] for piece in gu_pieces], "y", 1).reshape(2 * S * HP, DK)
    gu_all = lax.all_gather(gu_own, "expert", axis=0, tiled=True)
    down_all = lax.all_gather(sh_down_own, "expert", axis=0, tiled=True)

    grad_b = net.ring_gather(residual_grad.astype(BF16), "y")
    grad_b = jnp.stack(grad_b, axis=0).reshape(S * T, D)
    output_part = dot_tl(attended, grad_b)
    attended_grad = dot_tr(grad_b, w_output).astype(BF16).reshape(S, T, HL, VDIM)
    value_grad = einsum("bhts,bthd->bshd", probs_b, attended_grad)
    probs_grad = einsum("bthd,bshd->bhts", attended_grad, value_b)
    center = jnp.sum(probs * probs_grad, axis=-1, keepdims=True)
    output_part = after(output_part, gu_all, down_all).astype(BF16)
    output_w = lax.psum(output_part, "expert")
    scores_grad = (after(probs, output_part) * (probs_grad - center) * att_scale).astype(BF16)
    query_grad = einsum("bhts,bshd->bthd", scores_grad, key_b)
    key_grad = einsum("bhts,bthd->bshd", scores_grad, query_b)
    query_turn_grad = unrotate(
        query_grad[..., NOPE:], cosine[:, :, None, :], sine_table[:, :, None, :]
    )
    query_grad_b = (
        jnp.concatenate([query_grad[..., :NOPE], query_turn_grad], axis=-1)
        .astype(BF16)
        .reshape(S * T, HQ)
    )
    query_grad_all = gather_cols(query_grad_b, HQ)
    if not out_sums:
        for r in range(early, nr):
            out_work(r)(query_grad_b)
        out_sum_work(())
    keyval_grad_b = (
        jnp.concatenate([key_grad[..., :NOPE], value_grad], axis=-1)
        .astype(BF16)
        .reshape(S * T, HV)
    )
    latent_part = dot_tr(keyval_grad_b, keyval_full).reshape(S, T, KVR)
    rope_part = jnp.sum(key_grad[..., NOPE:], axis=2)
    latent_sum = block_all_sum(jnp.concatenate([latent_part, rope_part], axis=-1))
    latent_up = latent_sum[..., :KVR]
    key_rope_grad = unrotate(latent_sum[..., KVR:], cosine, sine_table)
    plain_latent = latent * scale_latent
    latent_gain_part = jnp.sum(latent_up * plain_latent, axis=(0, 1))
    inner_latent = latent_up * latent_gain_full
    latent_grad = scale_latent * (
        inner_latent - plain_latent * jnp.mean(inner_latent * plain_latent, axis=-1, keepdims=True)
    )
    latent_all_grad = (
        jnp.concatenate([latent_grad, key_rope_grad], axis=-1).astype(BF16).reshape(S * T, -1)
    )
    normed_grad = dot_tr(query_grad_all, w_query) + dot_tr(latent_all_grad, w_latent)
    plain_flat = plain_one.reshape(S * T, DK)
    attn_gain_part = jnp.sum(normed_grad * plain_flat, axis=0)
    inner_one = own_cols((normed_grad * attn_gain_f).reshape(S, T, DK))
    plain_own = inputs * scale_one
    tokens_grad = residual_grad + scale_one * (
        inner_one - plain_own * jnp.mean(inner_one * plain_own, axis=-1, keepdims=True)
    )

    query_part = dot_tl(normed_one, query_grad_all).astype(BF16)
    ffn_part, router_part = after((ffn_gain_part, router_grad_part), query_part)
    small_ffn = cols(ffn_part, s, DK)
    small_router = cols(router_part.T, s, DK)
    for r in range(1, S):
        sent = jnp.concatenate(
            [cols(ffn_part, s + r, DK)[None], cols(router_part.T, s + r, DK)], axis=0
        )
        got = net.hop(sent, "y", r)
        small_ffn = small_ffn + got[0]
        small_router = small_router + got[1:]
    latent_rows = dot_tl(latent_all_grad, normed_one).astype(BF16)
    small = jnp.concatenate(
        [
            attn_gain_part[None],
            small_ffn[None],
            jnp.pad(cols(latent_gain_part, s, KR), (0, DK - KR))[None],
            small_router,
        ],
        axis=0,
    )
    LW = latent_rows.shape[0]
    xz = ("c", "x", "z")
    output_w = output_w.astype(F32)
    tot_q, tot_l = lax.psum((query_part, latent_rows), "expert")
    tot_s = small
    for axis in "cxz":
        pieces = net.ring_gather(tot_s, axis)
        tot_s = functools.reduce(jnp.add, pieces)

    row_ids = after(jnp.arange(E * 2 * S * HP, dtype=jnp.int32), query_part)
    at_hidden = (
        ((row_ids // (HP * S)) % 2) * (S * HID)
        + ((row_ids // HP) % S) * HID
        + (row_ids // (HP * S * 2)) * HS
        + row_ids % HP
    )
    at_hidden = jnp.where(row_ids % HP < HS, at_hidden, -1)
    hidden_ids = jnp.arange(S * HID, dtype=jnp.int32)
    shared_gate_w = dot_tl(gu_all, (at_hidden[:, None] == hidden_ids[None]).astype(BF16))
    shared_up_w = dot_tl(gu_all, (at_hidden[:, None] == S * HID + hidden_ids[None]).astype(BF16))
    row_ids = after(jnp.arange(E * HP, dtype=jnp.int32), query_part)
    at_hidden = jnp.where(row_ids % HP < HS, (row_ids // HP) * HS + row_ids % HP, -1)
    place_down = (jnp.arange(HID, dtype=jnp.int32)[:, None] == at_hidden[None]).astype(BF16)
    shared_down_w = dot(place_down, down_all)

    def keyval_steps():
        piece = dot_tl(keyval_grad_b, latent_normed.reshape(S * T, KVR))
        piece = after(piece, query_part).astype(BF16)
        piece = yield from net.reduce_steps(piece, xz)
        mine = [cols(piece, s, KR)] + [None] * (S - 1)
        for r in range(1, S):
            mine[S - r] = net.hop(cols(piece, s + r, KR), "y", r)
        mine = net.absolute([p[None] for p in mine], "y", 0)
        value = yield from net.spread_steps(mine, xz, dim=1)
        return value

    out_1, out_2 = [v[0] for v in out_sums], [v[1] for v in out_sums]
    split = lambda v: [v[k] for k in range(v.shape[0])]
    got = net.scatter_stage(
        [split(v) for v in out_1] + [out_2],
        ("x",) * (len(out_1) + 1),
        [lambda marks: query_part] + [None] * (nx - 2),
    )
    one, two = net.scatter_stage([got[:-1], split(got[-1])], ("y", "y"))
    one = [jnp.concatenate([one[k], two[k]], axis=0) for k in range(nz)]
    routed = net.scatter_stage([one], ("z",))[0].astype(F32)
    (kv_all,) = net.in_rounds([keyval_steps()])
    block_out = (residual + routed).astype(BF16)
    keyval_w = dot_tr(jnp.eye(KR, dtype=BF16), kv_all.reshape(S * HV, KR))
    query_w = tot_q.astype(F32)
    latent_w = tot_l.astype(F32).T
    return (
        block_out,
        tokens_grad,
        tot_s[0],
        query_w,
        latent_w,
        tot_s[2, :KR],
        keyval_w,
        output_w,
        tot_s[1],
        tot_s[3:].T,
        shared_gate_w,
        shared_up_w,
        shared_down_w,
        gate_w_grad.T[None],
        up_w_grad.T[None],
        down_grad[None],
    )


def solution(mesh):
    both = P(("expert", "shard"), None)
    row = P("shard", None)
    in_specs = (
        both, both, both, P("shard"), row, row, P("shard"), row, row, P("shard"), row, row, row, row,
        P("expert", None, "shard"), P("expert", None, "shard"), P("expert", "shard", None), both,
    )
    out_specs = (
        both, both, P("shard"), row, row, P("shard"), row, row, P("shard"), row, row, row, row,
        P("expert", None, "shard"), P("expert", None, "shard"), P("expert", "shard", None),
    )
    return jax.shard_map(body, mesh=mesh, in_specs=in_specs, out_specs=out_specs, check_vma=False)
```

time: 2430 us -> 930 us (0.38)
  waiting for transfers between devices: 1670 us -> 315 us
  blocking collectives: 293 us -> 0 us
  Pallas kernels: 0 us -> 202 us
  matrix products: 262 us -> 96 us
  other arithmetic: 33.6 us -> 91.1 us
  starting transfers between devices: 18.2 us -> 68.5 us
  between operations: 16.8 us -> 51.1 us
  local copies, waits for them, and re-layouts: 126 us -> 94.6 us
    all_gather x16 -> x3, waiting for transfers between devices: 669 us -> 0.02 us  [the longest x1 0.02 us: body(): gu_all = lax.all_gather(gu_own, 'expert', axis=0, tiled=True)]
    psum x1, waiting for transfers between devices: 652 us -> 87.2 us  [body(): tot_q, tot_l = lax.psum((query_part, latent_rows), 'expert')]
    reduce_scatter x2 -> x0, waiting for transfers between devices: 247 us -> none  [the longest x1 140 us: body(): lax.psum_scatter((trail_product(pre_gate_grad, gate_local) + trail_produc...]
    ppermute x0 -> x68, waiting for transfers between devices: none -> 228 us  [the longest x47 156 us: hop(): return lax.ppermute(value, 'expert', pairs)]
    pallas_call x0 -> x8, Pallas kernels: none -> 202 us  [the longest x2 85.5 us: chain_call(): pl.pallas_call(functools.partial(chain_kernel, arrays, th, nz, routed, 25...]
    dot_general x39 -> x25, matrix products: 262 us -> 93.1 us  [the longest x7 39.9 us: dot_tl(): lax.dot_general(a, b, (((0,), (0,)), ((), ())), preferred_element_type=F32)]
    all_to_all x1 -> x0, blocking collectives: 166 us -> none  [body(): lax.all_to_all(send_grads, 'expert', split_axis=0, concat_axis=0, tiled=T...]
    all_to_all x3 -> x0, waiting for transfers between devices: 96 us -> none  [the longest x1 95.9 us: body(): lax.all_to_all(send_rows, 'expert', split_axis=0, concat_axis=0, tiled=True)]
  transfers between devices with their start and end apart: 22 -> 72, of which waited for: 15 -> 33; matrix products, arithmetic and copies ran while one was open for 14% -> 26% of each run, Pallas kernels for 0% -> 15%
where the time goes in v1:
time: 930 us; the launch traced here: 918 us
  waiting for transfers between devices  315 us (34%)
  Pallas kernels  202 us (22%)
  matrix products  96 us (10%)
  local copies, waits for them, and re-layouts  94.6 us (10%)
  other arithmetic  91.1 us (10%)
  starting transfers between devices  68.5 us (7%)
  between operations  51.1 us (5%)
    ppermute x47, waiting for transfers between devices, hop(): return lax.ppermute(value, 'expert', pairs)  156 us
    psum x1, waiting for transfers between devices, body(): tot_q, tot_l = lax.psum((query_part, latent_rows), 'expert')  87.2 us
    pallas_call x2, Pallas kernels, chain_call(): pl.pallas_call(functools.partial(chain_kernel, arrays, th, nz, routed, 25...  85.5 us
    ppermute x21, waiting for transfers between devices, hop(): return lax.ppermute(value, 'shard', [(i, (i + k) % n) for i in range(n)])  72 us
    pallas_call x3, Pallas kernels, weight_call(): pl.pallas_call(functools.partial(weight_kernel, calls, per, outs_n, hid,...  62.7 us
    ppermute x47, starting transfers between devices, hop(): return lax.ppermute(value, 'expert', pairs)  50.1 us
    dot_general x7, matrix products, dot_tl(): lax.dot_general(a, b, (((0,), (0,)), ((), ())), preferred_element_type=F32)  39.9 us
    convert_element_type x18, other arithmetic, add_b(): return (a.astype(F32) + b.astype(F32)).astype(BF16)  32.4 us
  transfers between devices with their start and end apart: 72, of which 33 were waited for; matrix products, arithmetic and copies ran while one was open for 26% of the time, Pallas kernels for 15%

profile of v1, /device:TPU:0, one launch (start us, length us, event | category | flops | bytes accessed | tf_op | source)
XLA Modules:
  0.0 917.9 jit_solution(798397449728203635)
XLA Ops:
  31.1 3.9 fusion.16
  50.6 24.8 %collective-permute-done.6 = bf16[2,48,1024]{2,1,0:T(8,128)(2,1)S(1)} collective-permute-done((bf16[2,48,1024]{2,1,0:T(8,128)(2,1)S(1)}, bf16[2,48,1024]{2,1,0:T(8,128)(2,1)S(1)}, u32[]{:S(2)}, u32[]{:S(2)}) %collective-permute-start.6) | collective-permute-done | bytes 196640 | tf_op jit(solution)/shard_map/ppermute | solution.py:76
  77.8 11.1 %collective-permute-done.4 = bf16[128,2048]{1,0:T(8,128)(2,1)S(1)} collective-permute-done((bf16[128,2048]{1,0:T(8,128)(2,1)}, bf16[128,2048]{1,0:T(8,128)(2,1)S(1)}, u32[]{:S(2)}, u32[]{:S(2)}) %collective-permute-start.4) | collective-permute-done | bytes 524320 | tf_op jit(solution)/shard_map/ppermute | solution.py:76
  95.5 4.4 convert_add_fusion.5
  118.0 3.7 fusion.76
  122.7 13.1 %collective-permute-done.8 = bf16[128,2048]{1,0:T(8,128)(2,1)S(1)} collective-permute-done((bf16[128,2048]{1,0:T(8,128)(2,1)S(1)}, bf16[128,2048]{1,0:T(8,128)(2,1)S(1)}, u32[]{:S(2)}, u32[]{:S(2)}) %collective-permute-start.8) | collective-permute-done | bytes 524320 | tf_op jit(solution)/shard_map/ppermute | solution.py:76
  140.5 7.7 collective-permute-done.14
  148.2 5.6 collective-permute-done.9
  154.1 5.3 collective-permute-done.15
  159.5 5.6 collective-permute-done.10
  165.2 5.5 collective-permute-done.16
  178.8 25.6 %down_rows.1 = (bf16[16,256,2048]{2,1,0:T(8,128)(2,1)}, f32[16,256,768]{2,1,0:T(8,128)}, bf16[16,256,128]{2,1,0:T(8,128)(2,1)S(1)}) custom-call(s32[8,16]{1,0:T(8,128)S(1)} %stack.146.tab, bf16[32,2,64,2176]{3,2,1,0:T(8,128)(2,1)} %bitcast.297, bf16[32,2,64,2176]{3,2,1,0:T(8,128)(2,1)} %bitcast.298, bf16[32,2,64,2176]{3,2,1,0:T(8,128)(2,1)} %bitcast.299, ...), custom_call_target="tpu_custom_call" | custom-call | flops 12884901888 | bytes 49283072 | tf_op jit(solution)/shard_map/down_rows/pallas_call | solution.py:266
  217.6 42.5 %expert_chain.2 = (bf16[2,4,64,2176]{3,2,1,0:T(8,128)(2,1)}, bf16[2,4,64,2176]{3,2,1,0:T(8,128)(2,1)}, bf16[2,4,64,2176]{3,2,1,0:T(8,128)(2,1)}, bf16[2,4,64,217...) custom-call(s32[6,8]{1,0:T(8,128)} %concatenate.229.tab, ...), custom_call_target="tpu_custom_call" | custom-call | flops 25769803776 | bytes 47185920 | tf_op jit(solution)/shard_map/expert_chain/pallas_call | solution.py:373
  273.0 43.0 %expert_chain.3 = (bf16[2,4,64,2176]{3,2,1,0:T(8,128)(2,1)}, bf16[2,4,64,2176]{3,2,1,0:T(8,128)(2,1)}, bf16[2,4,64,2176]{3,2,1,0:T(8,128)(2,1)}, bf16[2,4,64,217...) custom-call(s32[6,8]{1,0:T(8,128)} %broadcast_add_fusion.5.tab, ...), custom_call_target="tpu_custom_call" | custom-call | flops 25769803776 | bytes 47185920 | tf_op jit(solution)/shard_map/expert_chain/pallas_call | solution.py:373
  317.1 3.5 collective-permute-done.24
  320.6 3.7 add_convert_fusion.5
  334.1 20.8 %expert_weights.3 = (f32[704,2048]{1,0:T(8,128)}, f32[44,2048]{1,0:T(8,128)}) custom-call(f32[8,128]{1,0:T(8,128)} %add.969.tie_ref, bf16[4,512,768]{2,1,0:T(8,128)(2,1)} %bitcast.376, bf16[4,512,768]{2,1,0:T(8,128)(2,1)} %bitcast.378, bf16[4,512,2048]{2,1,0:T(8,128)(2,1)} %bitcast.367, bf16[4,512,2048]{2,1,0:T(8,128)(2,1)} %bitcast.369), custom_call_target="tpu_custom_call" | custom-call | flops 12884901888 | bytes 28835840 | tf_op jit(solution)/shard_map/expert_weights/pallas_call | solution.py:495
  358.0 21.1 %expert_weights.4 = (f32[704,2048]{1,0:T(8,128)}, f32[44,2048]{1,0:T(8,128)}) custom-call(f32[8,128]{1,0:T(8,128)} %add.970.tie_ref, bf16[4,512,768]{2,1,0:T(8,128)(2,1)} %bitcast.375, bf16[4,512,768]{2,1,0:T(8,128)(2,1)} %bitcast.377, bf16[4,512,2048]{2,1,0:T(8,128)(2,1)} %bitcast.368, bf16[4,512,2048]{2,1,0:T(8,128)(2,1)} %bitcast.370), custom_call_target="tpu_custom_call" | custom-call | flops 12884901888 | bytes 28835840 | tf_op jit(solution)/shard_map/expert_weights/pallas_call | solution.py:495
  396.2 20.9 %expert_weights.5 = (f32[704,2048]{1,0:T(8,128)}, f32[44,2048]{1,0:T(8,128)}) custom-call(f32[8,128]{1,0:T(8,128)} %add.979.tie_ref, bf16[4,512,768]{2,1,0:T(8,128)(2,1)} %bitcast.366, bf16[4,512,768]{2,1,0:T(8,128)(2,1)} %bitcast.374, bf16[8,512,2048]{2,1,0:T(8,128)(2,1)} %bitcast.358, bf16[8,512,2048]{2,1,0:T(8,128)(2,1)} %bitcast.359), custom_call_target="tpu_custom_call" | custom-call | flops 12884901888 | bytes 28835840 | tf_op jit(solution)/shard_map/expert_weights/pallas_call | solution.py:495
  421.9 5.8 collective-permute-done.38
  431.6 17.4 %collective-permute-done.27 = bf16[4,64,2176]{2,1,0:T(8,128)(2,1)} collective-permute-done((bf16[4,64,2176]{2,1,0:T(8,128)(2,1)}, bf16[4,64,2176]{2,1,0:T(8,128)(2,1)}, u32[]{:S(2)}, u32[]{:S(2)}) %collective-permute-start.27) | collective-permute-done | bytes 1114144 | tf_op jit(solution)/shard_map/ppermute | solution.py:82
  456.6 13.8 %expert_out.2 = (bf16[2,4,64,2048]{3,2,1,0:T(8,128)(2,1)S(1)}, bf16[2,4,64,2048]{3,2,1,0:T(8,128)(2,1)}, bf16[2,4,64,2048]{3,2,1,0:T(8,128)(2,1)}, bf16[2,4,64,2048]{3,2,1,0:T(8,128)(2,1)}) custom-call(s32[5,8]{1,0:T(8,128)S(1)} %broadcast_add_fusion.4.tab, bf16[8,256,768]{2,1,0:T(8,128)(2,1)} %get-tuple-element.53.gh_ref, bf16[704,2048]{1,0:T(8,128)(2,1)} %bitcast.294, ...), custom_call_target="tpu_custom_call" | custom-call | flops 6442450944 | bytes 14680064 | tf_op jit(solution)/shard_map/expert_out/pallas_call | solution.py:427
  478.8 14.2 %expert_out.3 = (bf16[2,4,64,2048]{3,2,1,0:T(8,128)(2,1)S(1)}, bf16[2,4,64,2048]{3,2,1,0:T(8,128)(2,1)}, bf16[2,4,64,2048]{3,2,1,0:T(8,128)(2,1)}, bf16[2,4,64,2048]{3,2,1,0:T(8,128)(2,1)}) custom-call(s32[5,8]{1,0:T(8,128)S(1)} %broadcast_add_fusion.3.tab, bf16[8,256,768]{2,1,0:T(8,128)(2,1)} %get-tuple-element.68.gh_ref, bf16[704,2048]{1,0:T(8,128)(2,1)} %bitcast.295, ...), custom_call_target="tpu_custom_call" | custom-call | flops 6442450944 | bytes 14680064 | tf_op jit(solution)/shard_map/expert_out/pallas_call | solution.py:427
  499.1 5.8 collective-permute-done.34
  517.8 14.0 %collective-permute-done.35 = bf16[128,2176]{1,0:T(8,128)(2,1)S(1)} collective-permute-done((bf16[128,2176]{1,0:T(8,128)(2,1)S(1)}, bf16[128,2176]{1,0:T(8,128)(2,1)S(1)}, u32[]{:S(2)}, u32[]{:S(2)}) %collective-permute-start.35) | collective-permute-done | bytes 557088 | tf_op jit(solution)/shard_map/ppermute | solution.py:82
  539.4 3.9 collective-permute-done.37
  562.6 4.1 convolution_bitcast_fusion.1
  569.1 4.2 convolution_bitcast_fusion
  604.8 10.5 %collective-permute-done.39 = bf16[2,128,1536]{2,1,0:T(8,128)(2,1)} collective-permute-done((bf16[2,128,1536]{2,1,0:T(8,128)(2,1)}, bf16[2,128,1536]{2,1,0:T(8,128)(2,1)}, u32[]{:S(2)}, u32[]{:S(2)}) %collective-permute-start.39) | collective-permute-done | bytes 786464 | tf_op jit(solution)/shard_map/ppermute | solution.py:76
  616.5 6.2 bitcast_convert_fusion
  639.4 3.5 add_convert_fusion.8
  644.3 5.6 fusion.36
  651.6 13.2 %fusion.2 = f32[1024,1408]{1,0:T(8,128)} fusion(bf16[3072,1024]{1,0:T(8,128)(2,1)S(1)} %bitcast.361, s32[3072]{0:T(1024)S(1)} %fusion.119), kind=kOutput, calls=%fused_computation.3 | convolution fusion | flops 8862695424 | bytes 12070912 | tf_op jit(solution)/shard_map/dot_general | solution.py:29
  664.8 12.8 %fusion.3 = f32[1024,1408]{1,0:T(8,128)} fusion(bf16[3072,1024]{1,0:T(8,128)(2,1)S(1)} %bitcast.361, s32[1408]{0:T(1024)S(1)} %copy-done.108, s32[3072]{0:T(1024)S(1)} %fusion.119), kind=kOutput, calls=%fused_computation.4 | convolution fusion | flops 8862695424 | bytes 12076544 | tf_op jit(solution)/shard_map/dot_general | solution.py:29
  677.9 5.0 fusion.21
  683.6 4.5 collective-permute-done.53
  696.0 9.5 %collective-permute-done.58 = bf16[512,512]{1,0:T(8,128)(2,1)S(1)} collective-permute-done((bf16[512,512]{1,0:T(8,128)(2,1)S(1)}, bf16[512,512]{1,0:T(8,128)(2,1)S(1)}, u32[]{:S(2)}, u32[]{:S(2)}) %collective-permute-start.58) | collective-permute-done | bytes 524320 | tf_op jit(solution)/shard_map/ppermute | solution.py:82
  710.7 6.2 collective-permute-done.59
  716.9 3.3 collective-permute-start.46
  723.6 16.8 %collective-permute-start.55 = (f32[19,1024]{1,0:T(8,128)S(1)}, f32[19,1024]{1,0:T(8,128)S(1)}, u32[]{:S(2)}, u32[]{:S(2)}) collective-permute-start(f32[19,1024]{1,0:T(8,128)S(1)} %collective-permute-done.54), channel_id=1, source_target_pairs={{0,8},{2,10},{4,12},{6,14},{8,16},{10,18},{12,20},{14,22},{16,24},... | collective-permute-start | bytes 233480 | tf_op jit(solution)/shard_map/ppermute | solution.py:82
  740.5 3.8 collective-permute-start.64
  745.1 6.4 collective-permute-done.63
  751.5 27.7 %collective-permute-done.64 = bf16[2,128,256]{2,1,0:T(8,128)(2,1)S(1)} collective-permute-done((bf16[2,128,256]{2,1,0:T(8,128)(2,1)S(1)}, bf16[2,128,256]{2,1,0:T(8,128)(2,1)S(1)}, u32[]{:S(2)}, u32[]{:S(2)}) %collective-permute-start.64) | collective-permute-done | bytes 131104 | tf_op jit(solution)/shard_map/ppermute | solution.py:82
  784.4 4.2 collective-permute-done.66
  790.8 12.2 %collective-permute-done.48 = bf16[128,2048]{1,0:T(8,128)(2,1)S(1)} collective-permute-done((bf16[128,2048]{1,0:T(8,128)(2,1)S(1)}, bf16[128,2048]{1,0:T(8,128)(2,1)S(1)}, u32[]{:S(2)}, u32[]{:S(2)}) %collective-permute-start.48) | collective-permute-done | bytes 524320 | tf_op jit(solution)/shard_map/ppermute | solution.py:82
  808.1 87.2 %all-reduce.15.cloned.1.call-done = (bf16[1024,3072]{1,0:T(8,128)(2,1)}, bf16[1024,576]{0,1:T(8,128)(2,1)}, bf16[1024,2048]{1,0:T(8,128)(2,1)}) async-done(((bf16[1024,3072]{1,0:T(8,128)(2,1)}, bf16[1024,576]{0,1:T(8,128)(2,1)}, bf16[1024,2048]{1,0:T(8,128)(2,1)}), (bf16[1024,3072]{1,0:T(8,128)(2,1)}, bf16[1024,576]{0,1:T(8,128)(2,1)}, bf16[1024,2048]{1,0:T(8,128)(2,1)})) %all-reduce.15.cloned.1.call-update) | async-done | bytes 11665424 | tf_op jit(solution)/shard_map/psum | solution.py:906
  895.3 9.4 %convert_element_type.831 = f32[1024,3072]{1,0:T(8,128)} convert(bf16[1024,3072]{1,0:T(8,128)(2,1)} %get-tuple-element.88) | non-fusion elementwise | flops 3145728 | bytes 18874368 | tf_op jit(solution)/shard_map/convert_element_type | solution.py:952
  904.7 4.5 convert_element_type.846
  (633 shorter events, 259.2 us)
Async XLA Ops:
  7.3 171.5 %all-gather.9.cloned.1.call-start = ((), (), s32[]{:S(2)}) async-start(), calls=%async_computation.2 | async-start | bytes 18382848 | tf_op jit(solution)/shard_map/all_gather | solution.py:700
  10.8 540.1 %all-gather.7.cloned.1.call-start = ((), (), s32[]{:S(2)}) async-start(), calls=%async_computation.1 | async-start | bytes 3342336 | tf_op jit(solution)/shard_map/all_gather | solution.py:827
  11.7 18.2 %collective-permute-start = (bf16[128,1024]{1,0:T(8,128)(2,1)}, bf16[128,1024]{1,0:T(8,128)(2,1)}, u32[]{:S(2)}, u32[]{:S(2)}) collective-permute-start(bf16[128,1024]{1,0:T(8,128)(2,1)} %get-tuple-element.147), channel_id=1, source_target_pairs={{0,1},{1,0},{2,3},{3,2},{4,5},{5,4},{6,7},{7,6},{8,9},{9,8},{10,11... | collective-permute-start | bytes 786440 | tf_op jit(solution)/shard_map/ppermute | solution.py:76
  36.2 52.9 %collective-permute-start.7 = (bf16[2,128,1536]{2,1,0:T(8,128)(2,1)}, bf16[2,128,1536]{2,1,0:T(8,128)(2,1)S(1)}, u32[]{:S(2)}, u32[]{:S(2)}) collective-permute-start(bf16[2,128,1536]{2,1,0:T(8,128)(2,1)} %bitcast.11), channel_id=1, source_target_pairs={{0,1},{1,0},{2,3},{3,2},{4,5},{5,4},{6,7},{7,6},{8,9},{9,8},{10,11... | collective-permute-start | bytes 2359304 | tf_op jit(solution)/shard_map/ppermute | solution.py:76
  39.7 37.6 %collective-permute-start.2 = (bf16[2,128,576]{1,2,0:T(8,128)(2,1)}, bf16[2,128,576]{1,2,0:T(8,128)(2,1)S(1)}, u32[]{:S(2)}, u32[]{:S(2)}) collective-permute-start(bf16[2,128,576]{1,2,0:T(8,128)(2,1)} %get-tuple-element.178), channel_id=1, source_target_pairs={{0,1},{1,0},{2,3},{3,2},{4,5},{5,4},{6,7},{7,6},{8,9},{9,8},{10,11... | collective-permute-start | bytes 884744 | tf_op jit(solution)/shard_map/ppermute | solution.py:76
  44.4 31.0 %collective-permute-start.6 = (bf16[2,48,1024]{2,1,0:T(8,128)(2,1)S(1)}, bf16[2,48,1024]{2,1,0:T(8,128)(2,1)S(1)}, u32[]{:S(2)}, u32[]{:S(2)}) collective-permute-start(bf16[2,48,1024]{2,1,0:T(8,128)(2,1)S(1)} %fusion.107), channel_id=1, source_target_pairs={{0,1},{1,0},{2,3},{3,2},{4,5},{5,4},{6,7},{7,6},{8,9},{9,8},{10,11... | collective-permute-start | bytes 589832 | tf_op jit(solution)/shard_map/ppermute | solution.py:76
  48.5 40.4 %collective-permute-start.4 = (bf16[128,2048]{1,0:T(8,128)(2,1)}, bf16[128,2048]{1,0:T(8,128)(2,1)S(1)}, u32[]{:S(2)}, u32[]{:S(2)}) collective-permute-start(bf16[128,2048]{1,0:T(8,128)(2,1)} %dynamic-slice_add_fusion), channel_id=1, source_target_pairs={{0,1},{1,0},{2,3},{3,2},{4,5},{5,4},{6,7},{7,6},{8,9},{9,8},{10,11... | collective-permute-start | bytes 1572872 | tf_op jit(solution)/shard_map/ppermute | solution.py:76
  121.8 14.0 %collective-permute-start.8 = (bf16[128,2048]{1,0:T(8,128)(2,1)S(1)}, bf16[128,2048]{1,0:T(8,128)(2,1)S(1)}, u32[]{:S(2)}, u32[]{:S(2)}) collective-permute-start(bf16[128,2048]{1,0:T(8,128)(2,1)S(1)} %slice.621), channel_id=1, source_target_pairs={{0,1},{1,0},{2,3},{3,2},{4,5},{5,4},{6,7},{7,6},{8,9},{9,8},{10,11... | collective-permute-start | bytes 1572872 | tf_op jit(solution)/shard_map/ppermute | solution.py:76
  138.7 15.1 %collective-permute-start.9 = (bf16[64,2048]{1,0:T(8,128)(2,1)S(1)}, bf16[64,2048]{1,0:T(8,128)(2,1)S(1)}, u32[]{:S(2)}, u32[]{:S(2)}) collective-permute-start(bf16[64,2048]{1,0:T(8,128)(2,1)S(1)} %get-tuple-element.145), channel_id=1, source_target_pairs={{0,8},{2,10},{4,12},{6,14},{8,16},{10,18},{12,20},{14,22},{16,24},... | collective-permute-start | bytes 786440 | tf_op jit(solution)/shard_map/ppermute | solution.py:82
  172.2 34.2 %collective-permute-start.17 = (bf16[4,64,2048]{2,1,0:T(8,128)(2,1)}, bf16[4,64,2048]{2,1,0:T(8,128)(2,1)}, u32[]{:S(2)}, u32[]{:S(2)}) collective-permute-start(bf16[4,64,2048]{2,1,0:T(8,128)(2,1)} %get-tuple-element.126), channel_id=1, source_target_pairs={{0,1},{1,0},{2,3},{3,2},{4,5},{5,4},{6,7},{7,6},{8,9},{9,8},{10,11... | collective-permute-start | bytes 3145736 | tf_op jit(solution)/shard_map/ppermute | solution.py:76
  177.6 31.6 %collective-permute-start.12 = (bf16[4,64,2048]{2,1,0:T(8,128)(2,1)}, bf16[4,64,2048]{2,1,0:T(8,128)(2,1)}, u32[]{:S(2)}, u32[]{:S(2)}) collective-permute-start(bf16[4,64,2048]{2,1,0:T(8,128)(2,1)} %get-tuple-element.128), channel_id=1, source_target_pairs={{0,4},{2,6},{4,0},{6,2},{8,12},{10,14},{12,8},{14,10},{16,20},{18,... | collective-permute-start | bytes 3145736 | tf_op jit(solution)/shard_map/ppermute | solution.py:82
  216.3 47.9 %collective-permute-start.22 = (bf16[2,4,64,2048]{3,2,1,0:T(8,128)(2,1)}, bf16[2,4,64,2048]{3,2,1,0:T(8,128)(2,1)S(1)}, u32[]{:S(2)}, u32[]{:S(2)}) collective-permute-start(bf16[2,4,64,2048]{3,2,1,0:T(8,128)(2,1)} %pad_maximum_fusion.1.refs_2_), channel_id=1, source_target_pairs={{0,4},{2,6},{4,0},{6,2},{8,12},{10,14},{12,8},{14,10},{16,20},{18,... | collective-permute-start | bytes 6291464 | tf_op jit(solution)/shard_map/ppermute | solution.py:82
  217.1 47.7 %collective-permute-start.20 = (bf16[2,4,64,2048]{3,2,1,0:T(8,128)(2,1)}, bf16[2,4,64,2048]{3,2,1,0:T(8,128)(2,1)S(1)}, u32[]{:S(2)}, u32[]{:S(2)}) collective-permute-start(bf16[2,4,64,2048]{3,2,1,0:T(8,128)(2,1)} %pad_maximum_fusion.refs_0_), channel_id=1, source_target_pairs={{0,1},{1,0},{2,3},{3,2},{4,5},{5,4},{6,7},{7,6},{8,9},{9,8},{10,11... | collective-permute-start | bytes 6291464 | tf_op jit(solution)/shard_map/ppermute | solution.py:76
  316.6 65.0 %collective-permute-start.19 = (bf16[2,4,64,2176]{3,2,1,0:T(8,128)(2,1)}, bf16[2,4,64,2176]{3,2,1,0:T(8,128)(2,1)S(1)}, u32[]{:S(2)}, u32[]{:S(2)}) collective-permute-start(bf16[2,4,64,2176]{3,2,1,0:T(8,128)(2,1)} %get-tuple-element.52), channel_id=1, source_target_pairs={{0,2},{2,0},{4,6},{6,4},{8,10},{10,8},{12,14},{14,12},{16,18},{18,... | collective-permute-start | bytes 6684680 | tf_op jit(solution)/shard_map/ppermute | solution.py:82
  316.7 72.7 %collective-permute-start.28 = (bf16[2,4,64,2176]{3,2,1,0:T(8,128)(2,1)}, bf16[2,4,64,2176]{3,2,1,0:T(8,128)(2,1)}, u32[]{:S(2)}, u32[]{:S(2)}) collective-permute-start(bf16[2,4,64,2176]{3,2,1,0:T(8,128)(2,1)} %get-tuple-element.67), channel_id=1, source_target_pairs={{0,2},{2,0},{4,6},{6,4},{8,10},{10,8},{12,14},{14,12},{16,18},{18,... | collective-permute-start | bytes 6684680 | tf_op jit(solution)/shard_map/ppermute | solution.py:82
  325.5 56.0 %collective-permute-start.25 = (bf16[2,4,64,2176]{3,2,1,0:T(8,128)(2,1)}, bf16[2,4,64,2176]{3,2,1,0:T(8,128)(2,1)}, u32[]{:S(2)}, u32[]{:S(2)}) collective-permute-start(bf16[2,4,64,2176]{3,2,1,0:T(8,128)(2,1)} %add_convert_fusion.5), channel_id=1, source_target_pairs={{0,1},{1,0},{2,3},{3,2},{4,5},{5,4},{6,7},{7,6},{8,9},{9,8},{10,11... | collective-permute-start | bytes 6684680 | tf_op jit(solution)/shard_map/ppermute | solution.py:76
  330.1 59.3 %collective-permute-start.29 = (bf16[2,4,64,2176]{3,2,1,0:T(8,128)(2,1)}, bf16[2,4,64,2176]{3,2,1,0:T(8,128)(2,1)}, u32[]{:S(2)}, u32[]{:S(2)}) collective-permute-start(bf16[2,4,64,2176]{3,2,1,0:T(8,128)(2,1)} %add_convert_fusion.4), channel_id=1, source_target_pairs={{0,4},{2,6},{4,0},{6,2},{8,12},{10,14},{12,8},{14,10},{16,20},{18,... | collective-permute-start | bytes 6684680 | tf_op jit(solution)/shard_map/ppermute | solution.py:82
  418.8 134.6 %all-gather.5.cloned.1.call-start = ((), (), s32[]{:S(2)}) async-start(), calls=%async_computation | async-start | bytes 6684672 | tf_op jit(solution)/shard_map/all_gather | solution.py:826
  418.8 30.1 %collective-permute-start.27 = (bf16[4,64,2176]{2,1,0:T(8,128)(2,1)}, bf16[4,64,2176]{2,1,0:T(8,128)(2,1)}, u32[]{:S(2)}, u32[]{:S(2)}) collective-permute-start(bf16[4,64,2176]{2,1,0:T(8,128)(2,1)} %copy-done.52), channel_id=1, source_target_pairs={{0,4},{2,6},{4,0},{6,2},{8,12},{10,14},{12,8},{14,10},{16,20},{18,... | collective-permute-start | bytes 3342344 | tf_op jit(solution)/shard_map/ppermute | solution.py:82
  429.8 25.5 %collective-permute-start.32 = (bf16[4,64,2176]{2,1,0:T(8,128)(2,1)}, bf16[4,64,2176]{2,1,0:T(8,128)(2,1)S(1)}, u32[]{:S(2)}, u32[]{:S(2)}) collective-permute-start(bf16[4,64,2176]{2,1,0:T(8,128)(2,1)} %copy-done.53), channel_id=1, source_target_pairs={{0,1},{1,0},{2,3},{3,2},{4,5},{5,4},{6,7},{7,6},{8,9},{9,8},{10,11... | collective-permute-start | bytes 3342344 | tf_op jit(solution)/shard_map/ppermute | solution.py:76
  456.5 18.8 %collective-permute-start.33 = (bf16[128,2176]{1,0:T(8,128)(2,1)S(1)}, bf16[128,2176]{1,0:T(8,128)(2,1)S(1)}, u32[]{:S(2)}, u32[]{:S(2)}) collective-permute-start(bf16[128,2176]{1,0:T(8,128)(2,1)S(1)} %pad_maximum_fusion.11), channel_id=1, source_target_pairs={{0,8},{2,10},{4,12},{6,14},{8,16},{10,18},{12,20},{14,22},{16,24},... | collective-permute-start | bytes 1671176 | tf_op jit(solution)/shard_map/ppermute | solution.py:82
  472.2 34.1 %collective-permute-start.30 = (bf16[2,4,64,2048]{3,2,1,0:T(8,128)(2,1)}, bf16[2,4,64,2048]{3,2,1,0:T(8,128)(2,1)}, u32[]{:S(2)}, u32[]{:S(2)}) collective-permute-start(bf16[2,4,64,2048]{3,2,1,0:T(8,128)(2,1)} %get-tuple-element.72), channel_id=1, source_target_pairs={{0,2},{2,0},{4,6},{6,4},{8,10},{10,8},{12,14},{14,12},{16,18},{18,... | collective-permute-start | bytes 6291464 | tf_op jit(solution)/shard_map/ppermute | solution.py:82
  477.5 27.4 %collective-permute-start.34 = (bf16[128,2176]{1,0:T(8,128)(2,1)}, bf16[128,2176]{1,0:T(8,128)(2,1)}, u32[]{:S(2)}, u32[]{:S(2)}) collective-permute-start(bf16[128,2176]{1,0:T(8,128)(2,1)} %add_convert_fusion.17), channel_id=1, source_target_pairs={{0,8},{2,10},{4,12},{6,14},{8,16},{10,18},{12,20},{14,22},{16,24},... | collective-permute-start | bytes 1671176 | tf_op jit(solution)/shard_map/ppermute | solution.py:82
  494.3 18.7 %collective-permute-start.36 = (bf16[2,4,64,2048]{3,2,1,0:T(8,128)(2,1)}, bf16[2,4,64,2048]{3,2,1,0:T(8,128)(2,1)}, u32[]{:S(2)}, u32[]{:S(2)}) collective-permute-start(bf16[2,4,64,2048]{3,2,1,0:T(8,128)(2,1)} %get-tuple-element.74), channel_id=1, source_target_pairs={{0,2},{2,0},{4,6},{6,4},{8,10},{10,8},{12,14},{14,12},{16,18},{18,... | collective-permute-start | bytes 6291464 | tf_op jit(solution)/shard_map/ppermute | solution.py:82
  496.0 142.1 %collective-permute-start.42 = (bf16[2,4,64,2048]{3,2,1,0:T(8,128)(2,1)}, bf16[2,4,64,2048]{3,2,1,0:T(8,128)(2,1)}, u32[]{:S(2)}, u32[]{:S(2)}) collective-permute-start(bf16[2,4,64,2048]{3,2,1,0:T(8,128)(2,1)} %get-tuple-element.76), channel_id=1, source_target_pairs={{0,2},{2,0},{4,6},{6,4},{8,10},{10,8},{12,14},{14,12},{16,18},{18,... | collective-permute-start | bytes 6291464 | tf_op jit(solution)/shard_map/ppermute | solution.py:82
  499.0 36.2 %collective-permute-start.43 = (bf16[2,4,64,2048]{3,2,1,0:T(8,128)(2,1)}, bf16[2,4,64,2048]{3,2,1,0:T(8,128)(2,1)S(1)}, u32[]{:S(2)}, u32[]{:S(2)}) collective-permute-start(bf16[2,4,64,2048]{3,2,1,0:T(8,128)(2,1)} %get-tuple-element.78), channel_id=1, source_target_pairs={{0,2},{2,0},{4,6},{6,4},{8,10},{10,8},{12,14},{14,12},{16,18},{18,... | collective-permute-start | bytes 6291464 | tf_op jit(solution)/shard_map/ppermute | solution.py:82
  506.2 25.6 %collective-permute-start.35 = (bf16[128,2176]{1,0:T(8,128)(2,1)S(1)}, bf16[128,2176]{1,0:T(8,128)(2,1)S(1)}, u32[]{:S(2)}, u32[]{:S(2)}) collective-permute-start(bf16[128,2176]{1,0:T(8,128)(2,1)S(1)} %add_convert_fusion.16), channel_id=1, source_target_pairs={{0,8},{2,10},{4,12},{6,14},{8,16},{10,18},{12,20},{14,22},{16,24},... | collective-permute-start | bytes 1671176 | tf_op jit(solution)/shard_map/ppermute | solution.py:82
  512.4 180.7 %collective-permute-start.31 = (bf16[4,64,2048]{2,1,0:T(8,128)(2,1)}, bf16[4,64,2048]{2,1,0:T(8,128)(2,1)}, u32[]{:S(2)}, u32[]{:S(2)}) collective-permute-start(bf16[4,64,2048]{2,1,0:T(8,128)(2,1)} %slice_bitcast_fusion.8), channel_id=1, source_target_pairs={{0,4},{2,6},{4,0},{6,2},{8,12},{10,14},{12,8},{14,10},{16,20},{18,... | collective-permute-start | bytes 3145736 | tf_op jit(solution)/shard_map/ppermute | solution.py:82
  535.2 99.7 %collective-permute-start.40 = (bf16[4,64,2048]{2,1,0:T(8,128)(2,1)}, bf16[4,64,2048]{2,1,0:T(8,128)(2,1)}, u32[]{:S(2)}, u32[]{:S(2)}) collective-permute-start(bf16[4,64,2048]{2,1,0:T(8,128)(2,1)} %slice_bitcast_fusion.6), channel_id=1, source_target_pairs={{0,4},{2,6},{4,0},{6,2},{8,12},{10,14},{12,8},{14,10},{16,20},{18,... | collective-permute-start | bytes 3145736 | tf_op jit(solution)/shard_map/ppermute | solution.py:82
  537.7 101.6 %collective-permute-start.44 = (bf16[2,4,64,2048]{3,2,1,0:T(8,128)(2,1)}, bf16[2,4,64,2048]{3,2,1,0:T(8,128)(2,1)}, u32[]{:S(2)}, u32[]{:S(2)}) collective-permute-start(bf16[2,4,64,2048]{3,2,1,0:T(8,128)(2,1)} %add_convert_fusion.9), channel_id=1, source_target_pairs={{0,4},{2,6},{4,0},{6,2},{8,12},{10,14},{12,8},{14,10},{16,20},{18,... | collective-permute-start | bytes 6291464 | tf_op jit(solution)/shard_map/ppermute | solution.py:82
  595.6 19.7 %collective-permute-start.39 = (bf16[2,128,1536]{2,1,0:T(8,128)(2,1)}, bf16[2,128,1536]{2,1,0:T(8,128)(2,1)}, u32[]{:S(2)}, u32[]{:S(2)}) collective-permute-start(bf16[2,128,1536]{2,1,0:T(8,128)(2,1)} %copy.257), channel_id=1, source_target_pairs={{0,1},{1,0},{2,3},{3,2},{4,5},{5,4},{6,7},{7,6},{8,9},{9,8},{10,11... | collective-permute-start | bytes 2359304 | tf_op jit(solution)/shard_map/ppermute | solution.py:76
  623.9 271.4 %all-reduce.15.cloned.1.call-start = ((), (), s32[]{:S(2)}) async-start(), calls=%async_computation.3 | async-start | bytes 23330816 | tf_op jit(solution)/shard_map/psum | solution.py:906
  629.6 59.0 %collective-permute-start.57 = (bf16[1024,512]{1,0:T(8,128)(2,1)}, bf16[1024,512]{1,0:T(8,128)(2,1)}, u32[]{:S(2)}, u32[]{:S(2)}) collective-permute-start(bf16[1024,512]{1,0:T(8,128)(2,1)} %constant_dynamic-slice_fusion.6), channel_id=1, source_target_pairs={{0,2},{2,0},{4,6},{6,4},{8,10},{10,8},{12,14},{14,12},{16,18},{18,... | collective-permute-start | bytes 3145736 | tf_op jit(solution)/shard_map/ppermute | solution.py:82
  634.9 42.7 %collective-permute-start.51 = (f32[17,1024]{1,0:T(8,128)S(1)}, f32[17,1024]{1,0:T(8,128)S(1)}, u32[]{:S(2)}, u32[]{:S(2)}) collective-permute-start(f32[17,1024]{1,0:T(8,128)S(1)} %pad_maximum_fusion.20), channel_id=1, source_target_pairs={{0,1},{1,0},{2,3},{3,2},{4,5},{5,4},{6,7},{7,6},{8,9},{9,8},{10,11... | collective-permute-start | bytes 208904 | tf_op jit(solution)/shard_map/ppermute | solution.py:76
  638.0 55.1 %collective-permute-start.41 = (bf16[4,64,2048]{2,1,0:T(8,128)(2,1)S(1)}, bf16[4,64,2048]{2,1,0:T(8,128)(2,1)S(1)}, u32[]{:S(2)}, u32[]{:S(2)}) collective-permute-start(bf16[4,64,2048]{2,1,0:T(8,128)(2,1)S(1)} %fusion.23), channel_id=1, source_target_pairs={{0,1},{1,0},{2,3},{3,2},{4,5},{5,4},{6,7},{7,6},{8,9},{9,8},{10,11... | collective-permute-start | bytes 3145736 | tf_op jit(solution)/shard_map/ppermute | solution.py:76
  643.0 49.3 %collective-permute-start.45 = (bf16[4,64,2048]{2,1,0:T(8,128)(2,1)S(1)}, bf16[4,64,2048]{2,1,0:T(8,128)(2,1)S(1)}, u32[]{:S(2)}, u32[]{:S(2)}) collective-permute-start(bf16[4,64,2048]{2,1,0:T(8,128)(2,1)S(1)} %slice_bitcast_fusion.4), channel_id=1, source_target_pairs={{0,1},{1,0},{2,3},{3,2},{4,5},{5,4},{6,7},{7,6},{8,9},{9,8},{10,11... | collective-permute-start | bytes 3145736 | tf_op jit(solution)/shard_map/ppermute | solution.py:76
  688.1 35.1 %collective-permute-start.50 = (bf16[128,1024]{1,0:T(8,128)(2,1)S(1)}, bf16[128,1024]{1,0:T(8,128)(2,1)S(1)}, u32[]{:S(2)}, u32[]{:S(2)}) collective-permute-start(bf16[128,1024]{1,0:T(8,128)(2,1)S(1)} %get-tuple-element.138), channel_id=1, source_target_pairs={{0,1},{1,0},{2,3},{3,2},{4,5},{5,4},{6,7},{7,6},{8,9},{9,8},{10,11... | collective-permute-start | bytes 786440 | tf_op jit(solution)/shard_map/ppermute | solution.py:76
  688.6 35.0 %collective-permute-start.54 = (f32[19,1024]{1,0:T(8,128)S(1)}, f32[19,1024]{1,0:T(8,128)S(1)}, u32[]{:S(2)}, u32[]{:S(2)}) collective-permute-start(f32[19,1024]{1,0:T(8,128)S(1)} %add.1039), channel_id=1, source_target_pairs={{0,8},{2,10},{4,12},{6,14},{8,16},{10,18},{12,20},{14,22},{16,24},... | collective-permute-start | bytes 233480 | tf_op jit(solution)/shard_map/ppermute | solution.py:82
  706.8 15.1 %collective-permute-start.60 = (bf16[128,512]{1,0:T(8,128)(2,1)S(1)}, bf16[128,512]{1,0:T(8,128)(2,1)S(1)}, u32[]{:S(2)}, u32[]{:S(2)}) collective-permute-start(bf16[128,512]{1,0:T(8,128)(2,1)S(1)} %get-tuple-element.137), channel_id=1, source_target_pairs={{0,16},{2,18},{4,20},{6,22},{8,24},{10,26},{12,28},{14,30},{16,0},... | collective-permute-start | bytes 393224 | tf_op jit(solution)/shard_map/ppermute | solution.py:82
  708.0 13.9 %collective-permute-start.61 = (bf16[128,512]{1,0:T(8,128)(2,1)S(1)}, bf16[128,512]{1,0:T(8,128)(2,1)S(1)}, u32[]{:S(2)}, u32[]{:S(2)}) collective-permute-start(bf16[128,512]{1,0:T(8,128)(2,1)S(1)} %get-tuple-element.136), channel_id=1, source_target_pairs={{0,24},{2,26},{4,28},{6,30},{8,0},{10,2},{12,4},{14,6},{16,8},{18,... | collective-permute-start | bytes 393224 | tf_op jit(solution)/shard_map/ppermute | solution.py:82
  716.9 27.4 %collective-permute-start.46 = (bf16[128,2048]{1,0:T(8,128)(2,1)S(1)}, bf16[128,2048]{1,0:T(8,128)(2,1)S(1)}, u32[]{:S(2)}, u32[]{:S(2)}) collective-permute-start(bf16[128,2048]{1,0:T(8,128)(2,1)S(1)} %pad_maximum_fusion.13), channel_id=1, source_target_pairs={{0,8},{2,10},{4,12},{6,14},{8,16},{10,18},{12,20},{14,22},{16,24},... | collective-permute-start | bytes 1572872 | tf_op jit(solution)/shard_map/ppermute | solution.py:82
  722.0 18.4 %collective-permute-start.62 = (bf16[128,256]{1,0:T(8,128)(2,1)S(1)}, bf16[128,256]{1,0:T(8,128)(2,1)S(1)}, u32[]{:S(2)}, u32[]{:S(2)}) collective-permute-start(bf16[128,256]{1,0:T(8,128)(2,1)S(1)} %get-tuple-element.156), channel_id=1, source_target_pairs={{0,1},{1,0},{2,3},{3,2},{4,5},{5,4},{6,7},{7,6},{8,9},{9,8},{10,11... | collective-permute-start | bytes 196616 | tf_op jit(solution)/shard_map/ppermute | solution.py:76
  723.6 57.2 %collective-permute-start.55 = (f32[19,1024]{1,0:T(8,128)S(1)}, f32[19,1024]{1,0:T(8,128)S(1)}, u32[]{:S(2)}, u32[]{:S(2)}) collective-permute-start(f32[19,1024]{1,0:T(8,128)S(1)} %collective-permute-done.54), channel_id=1, source_target_pairs={{0,8},{2,10},{4,12},{6,14},{8,16},{10,18},{12,20},{14,22},{16,24},... | collective-permute-start | bytes 233480 | tf_op jit(solution)/shard_map/ppermute | solution.py:82
  740.5 38.7 %collective-permute-start.64 = (bf16[2,128,256]{2,1,0:T(8,128)(2,1)S(1)}, bf16[2,128,256]{2,1,0:T(8,128)(2,1)S(1)}, u32[]{:S(2)}, u32[]{:S(2)}) collective-permute-start(bf16[2,128,256]{2,1,0:T(8,128)(2,1)S(1)} %get-tuple-element.92), channel_id=1, source_target_pairs={{0,16},{2,18},{4,20},{6,22},{8,24},{10,26},{12,28},{14,30},{16,0},... | collective-permute-start | bytes 393224 | tf_op jit(solution)/shard_map/ppermute | solution.py:82
  744.5 37.3 %collective-permute-start.47 = (bf16[128,2048]{1,0:T(8,128)(2,1)S(1)}, bf16[128,2048]{1,0:T(8,128)(2,1)S(1)}, u32[]{:S(2)}, u32[]{:S(2)}) collective-permute-start(bf16[128,2048]{1,0:T(8,128)(2,1)S(1)} %add_convert_fusion.22), channel_id=1, source_target_pairs={{0,8},{2,10},{4,12},{6,14},{8,16},{10,18},{12,20},{14,22},{16,24},... | collective-permute-start | bytes 1572872 | tf_op jit(solution)/shard_map/ppermute | solution.py:82
  744.5 34.7 %collective-permute-start.65 = (bf16[2,128,256]{2,1,0:T(8,128)(2,1)S(1)}, bf16[2,128,256]{2,1,0:T(8,128)(2,1)S(1)}, u32[]{:S(2)}, u32[]{:S(2)}) collective-permute-start(bf16[2,128,256]{2,1,0:T(8,128)(2,1)S(1)} %get-tuple-element.92), channel_id=1, source_target_pairs={{0,8},{2,10},{4,12},{6,14},{8,16},{10,18},{12,20},{14,22},{16,24},... | collective-permute-start | bytes 393224 | tf_op jit(solution)/shard_map/ppermute | solution.py:82
  781.9 21.2 %collective-permute-start.48 = (bf16[128,2048]{1,0:T(8,128)(2,1)S(1)}, bf16[128,2048]{1,0:T(8,128)(2,1)S(1)}, u32[]{:S(2)}, u32[]{:S(2)}) collective-permute-start(bf16[128,2048]{1,0:T(8,128)(2,1)S(1)} %add_convert_fusion.21), channel_id=1, source_target_pairs={{0,8},{2,10},{4,12},{6,14},{8,16},{10,18},{12,20},{14,22},{16,24},... | collective-permute-start | bytes 1572872 | tf_op jit(solution)/shard_map/ppermute | solution.py:82
  788.9 15.9 %collective-permute-start.67 = (bf16[2,1024,256]{2,1,0:T(8,128)(2,1)S(1)}, bf16[2,1024,256]{2,1,0:T(8,128)(2,1)S(1)}, u32[]{:S(2)}, u32[]{:S(2)}) collective-permute-start(bf16[2,1024,256]{2,1,0:T(8,128)(2,1)S(1)} %maximum_select_fusion.7), channel_id=1, source_target_pairs={{0,2},{2,0},{4,6},{6,4},{8,10},{10,8},{12,14},{14,12},{16,18},{18,... | collective-permute-start | bytes 3145736 | tf_op jit(solution)/shard_map/ppermute | solution.py:82
  (158 other events, 1544.4 us)
Sparse Core Ops, SparseCore 0:
  11.5 127.7 all-gather.8
  418.9 49.8 all-gather.6
  471.1 81.5 all-gather.4
  629.8 265.4 all-reduce.14

commit v2 on v1

--- a/solution.py
+++ b/solution.py
@@ -621,9 +621,9 @@
     ]
     latent_part_own = dot(normed_one, w_latent).reshape(S, T, -1)
     latent_sent = latent_part_own.astype(BF16)
-    first = (query_parts, latent_sent)
     query_got = [net.hop(part, "y", r) for r, part in enumerate(query_parts, 1)]
     latent_got = [net.hop(latent_sent, "y", r) for r in range(1, S)]
+    first = query_got
     core = net.pos("c")
     half_rows = KR // net.n["c"]
     kv_half = lax.dynamic_slice_in_dim(w_keyval, core * half_rows, half_rows, 0)
@@ -653,7 +653,6 @@
     router_pad = jnp.pad(router_full.T, ((0, 0), (0, LANES - E)))
 
     queries = dot(normed_one, cols(w_query, s, HQ)).reshape(S, T, HQ)
-    queries = after(queries, sh_down, sh_slices, keyval_full)
     for r, got in enumerate(query_got, 1):
         queries = queries + jnp.concatenate([got[r:], got[:r]], axis=0).astype(F32)
     queries = queries.reshape(S, T, HL, NOPE + ROPE)
@@ -685,7 +684,8 @@
     raised = jnp.exp(scores - peak)
     probs = raised / jnp.sum(raised, axis=-1, keepdims=True)
     probs_b = probs.astype(BF16)
-    attended = einsum("bhts,bshd->bthd", probs_b, value_b).astype(BF16).reshape(S * T, HL * VDIM)
+    attended = einsum("bhts,bshd->bthd", probs_b, value_b)
+    attended = after(attended, sh_slices).astype(BF16).reshape(S * T, HL * VDIM)
     out_parts = dot(attended, w_output).reshape(S, T, D)
     residual = inputs + pair_sum_blocks([out_parts[r] for r in blocks])
     scale_two = norm_scale(residual)

time: 930 us -> 930 us (level)
  waiting for transfers between devices: 315 us -> 298 us
    ppermute x21, waiting for transfers between devices: 72 us -> 60.7 us  [hop(): return lax.ppermute(value, 'shard', [(i, (i + k) % n) for i in range(n)])]
    unnamed x282 -> x276, local copies, waits for them, and re-layouts: 21.1 us -> 27.5 us
    slice x24 -> x21, local copies, waits for them, and re-layouts: 21.2 us -> 18.8 us  [zero_of(): one = lax.slice(mark, (0,) * mark.ndim, (1,) * mark.ndim).reshape(())]
  transfers between devices with their start and end apart: 72 -> 72, of which waited for: 33 -> 33; matrix products, arithmetic and copies ran while one was open for 26% -> 28% of each run, Pallas kernels for 15% -> 15%
where the time goes in v2:
time: 930 us; the launch traced here: 918 us
  waiting for transfers between devices  298 us (32%)
  Pallas kernels  202 us (22%)
  local copies, waits for them, and re-layouts  101 us (11%)
  other arithmetic  99.1 us (11%)
  matrix products  94.8 us (10%)
  starting transfers between devices  77.2 us (8%)
  between operations  46.8 us (5%)
    ppermute x47, waiting for transfers between devices, hop(): return lax.ppermute(value, 'expert', pairs)  147 us
    psum x1, waiting for transfers between devices, body(): tot_q, tot_l = lax.psum((query_part, latent_rows), 'expert')  86.9 us
    pallas_call x2, Pallas kernels, chain_call(): pl.pallas_call(functools.partial(chain_kernel, arrays, th, nz, routed, 25...  85.4 us
    pallas_call x3, Pallas kernels, weight_call(): pl.pallas_call(functools.partial(weight_kernel, calls, per, outs_n, hid,...  62.8 us
    ppermute x21, waiting for transfers between devices, hop(): return lax.ppermute(value, 'shard', [(i, (i + k) % n) for i in range(n)])  60.7 us
    ppermute x47, starting transfers between devices, hop(): return lax.ppermute(value, 'expert', pairs)  51.8 us
    dot_general x7, matrix products, dot_tl(): lax.dot_general(a, b, (((0,), (0,)), ((), ())), preferred_element_type=F32)  39.9 us
    convert_element_type x18, other arithmetic, add_b(): return (a.astype(F32) + b.astype(F32)).astype(BF16)  32.1 us
  transfers between devices with their start and end apart: 72, of which 33 were waited for; matrix products, arithmetic and copies ran while one was open for 28% of the time, Pallas kernels for 15%

profile of v2, /device:TPU:0, one launch (start us, length us, event | category | flops | bytes accessed | tf_op | source)
XLA Modules:
  0.0 918.3 jit_solution(9446209638931675541)
XLA Ops:
  35.8 3.8 fusion.13
  46.9 20.5 %collective-permute-done.4 = bf16[2,128,1536]{2,1,0:T(8,128)(2,1)} collective-permute-done((bf16[2,128,1536]{2,1,0:T(8,128)(2,1)}, bf16[2,128,1536]{2,1,0:T(8,128)(2,1)}, u32[]{:S(2)}, u32[]{:S(2)}) %collective-permute-start.4) | collective-permute-done | bytes 786464 | tf_op jit(solution)/shard_map/ppermute | solution.py:76
  73.8 4.2 convert_add_fusion.5
  86.2 5.4 collective-permute-done.5
  93.7 4.6 collective-permute-done.7
  105.1 4.0 copy.244
  121.9 4.0 fusion.72
  126.6 8.9 collective-permute-done.8
  141.9 8.0 collective-permute-done.14
  151.2 4.5 collective-permute-done.9
  155.8 5.8 collective-permute-done.15
  161.6 5.5 collective-permute-done.10
  168.2 4.7 collective-permute-done.16
  179.8 25.6 %down_rows.1 = (bf16[16,256,2048]{2,1,0:T(8,128)(2,1)}, f32[16,256,768]{2,1,0:T(8,128)}, bf16[16,256,128]{2,1,0:T(8,128)(2,1)S(1)}) custom-call(s32[8,16]{1,0:T(8,128)S(1)} %stack.146.tab, bf16[32,2,64,2176]{3,2,1,0:T(8,128)(2,1)} %bitcast.293, bf16[32,2,64,2176]{3,2,1,0:T(8,128)(2,1)} %bitcast.294, bf16[32,2,64,2176]{3,2,1,0:T(8,128)(2,1)} %bitcast.295, ...), custom_call_target="tpu_custom_call" | custom-call | flops 12884901888 | bytes 49283072 | tf_op jit(solution)/shard_map/down_rows/pallas_call | solution.py:266
  218.7 42.6 %expert_chain.2 = (bf16[2,4,64,2176]{3,2,1,0:T(8,128)(2,1)}, bf16[2,4,64,2176]{3,2,1,0:T(8,128)(2,1)}, bf16[2,4,64,2176]{3,2,1,0:T(8,128)(2,1)}, bf16[2,4,64,217...) custom-call(s32[6,8]{1,0:T(8,128)} %concatenate.229.tab, ...), custom_call_target="tpu_custom_call" | custom-call | flops 25769803776 | bytes 47185920 | tf_op jit(solution)/shard_map/expert_chain/pallas_call | solution.py:373
  273.2 42.8 %expert_chain.3 = (bf16[2,4,64,2176]{3,2,1,0:T(8,128)(2,1)}, bf16[2,4,64,2176]{3,2,1,0:T(8,128)(2,1)}, bf16[2,4,64,2176]{3,2,1,0:T(8,128)(2,1)}, bf16[2,4,64,217...) custom-call(s32[6,8]{1,0:T(8,128)} %broadcast_add_fusion.5.tab, ...), custom_call_target="tpu_custom_call" | custom-call | flops 25769803776 | bytes 47185920 | tf_op jit(solution)/shard_map/expert_chain/pallas_call | solution.py:373
  317.1 3.5 collective-permute-done.24
  320.6 3.7 add_convert_fusion.5
  334.0 20.8 %expert_weights.3 = (f32[704,2048]{1,0:T(8,128)}, f32[44,2048]{1,0:T(8,128)}) custom-call(f32[8,128]{1,0:T(8,128)} %add.954.tie_ref, bf16[4,512,768]{2,1,0:T(8,128)(2,1)} %bitcast.369, bf16[4,512,768]{2,1,0:T(8,128)(2,1)} %bitcast.371, bf16[4,512,2048]{2,1,0:T(8,128)(2,1)} %bitcast.360, bf16[4,512,2048]{2,1,0:T(8,128)(2,1)} %bitcast.362), custom_call_target="tpu_custom_call" | custom-call | flops 12884901888 | bytes 28835840 | tf_op jit(solution)/shard_map/expert_weights/pallas_call | solution.py:495
  357.9 21.1 %expert_weights.4 = (f32[704,2048]{1,0:T(8,128)}, f32[44,2048]{1,0:T(8,128)}) custom-call(f32[8,128]{1,0:T(8,128)} %add.955.tie_ref, bf16[4,512,768]{2,1,0:T(8,128)(2,1)} %bitcast.368, bf16[4,512,768]{2,1,0:T(8,128)(2,1)} %bitcast.370, bf16[4,512,2048]{2,1,0:T(8,128)(2,1)} %bitcast.361, bf16[4,512,2048]{2,1,0:T(8,128)(2,1)} %bitcast.363), custom_call_target="tpu_custom_call" | custom-call | flops 12884901888 | bytes 28835840 | tf_op jit(solution)/shard_map/expert_weights/pallas_call | solution.py:495
  396.1 20.9 %expert_weights.5 = (f32[704,2048]{1,0:T(8,128)}, f32[44,2048]{1,0:T(8,128)}) custom-call(f32[8,128]{1,0:T(8,128)} %add.964.tie_ref, bf16[4,512,768]{2,1,0:T(8,128)(2,1)} %bitcast.359, bf16[4,512,768]{2,1,0:T(8,128)(2,1)} %bitcast.367, bf16[8,512,2048]{2,1,0:T(8,128)(2,1)} %bitcast.351, bf16[8,512,2048]{2,1,0:T(8,128)(2,1)} %bitcast.352), custom_call_target="tpu_custom_call" | custom-call | flops 12884901888 | bytes 28835840 | tf_op jit(solution)/shard_map/expert_weights/pallas_call | solution.py:495
  422.8 4.9 collective-permute-done.38
  432.6 16.7 %collective-permute-done.27 = bf16[4,64,2176]{2,1,0:T(8,128)(2,1)} collective-permute-done((bf16[4,64,2176]{2,1,0:T(8,128)(2,1)}, bf16[4,64,2176]{2,1,0:T(8,128)(2,1)}, u32[]{:S(2)}, u32[]{:S(2)}) %collective-permute-start.27) | collective-permute-done | bytes 1114144 | tf_op jit(solution)/shard_map/ppermute | solution.py:82
  456.5 13.8 %expert_out.2 = (bf16[2,4,64,2048]{3,2,1,0:T(8,128)(2,1)S(1)}, bf16[2,4,64,2048]{3,2,1,0:T(8,128)(2,1)}, bf16[2,4,64,2048]{3,2,1,0:T(8,128)(2,1)}, bf16[2,4,64,2048]{3,2,1,0:T(8,128)(2,1)}) custom-call(s32[5,8]{1,0:T(8,128)S(1)} %broadcast_add_fusion.4.tab, bf16[8,256,768]{2,1,0:T(8,128)(2,1)} %get-tuple-element.53.gh_ref, bf16[704,2048]{1,0:T(8,128)(2,1)} %bitcast.290, ...), custom_call_target="tpu_custom_call" | custom-call | flops 6442450944 | bytes 14680064 | tf_op jit(solution)/shard_map/expert_out/pallas_call | solution.py:427
  478.5 14.2 %expert_out.3 = (bf16[2,4,64,2048]{3,2,1,0:T(8,128)(2,1)S(1)}, bf16[2,4,64,2048]{3,2,1,0:T(8,128)(2,1)}, bf16[2,4,64,2048]{3,2,1,0:T(8,128)(2,1)}, bf16[2,4,64,2048]{3,2,1,0:T(8,128)(2,1)}) custom-call(s32[5,8]{1,0:T(8,128)S(1)} %broadcast_add_fusion.3.tab, bf16[8,256,768]{2,1,0:T(8,128)(2,1)} %get-tuple-element.68.gh_ref, bf16[704,2048]{1,0:T(8,128)(2,1)} %bitcast.291, ...), custom_call_target="tpu_custom_call" | custom-call | flops 6442450944 | bytes 14680064 | tf_op jit(solution)/shard_map/expert_out/pallas_call | solution.py:427
  498.8 5.8 collective-permute-done.34
  518.0 12.8 %collective-permute-done.35 = bf16[128,2176]{1,0:T(8,128)(2,1)S(1)} collective-permute-done((bf16[128,2176]{1,0:T(8,128)(2,1)S(1)}, bf16[128,2176]{1,0:T(8,128)(2,1)S(1)}, u32[]{:S(2)}, u32[]{:S(2)}) %collective-permute-start.35) | collective-permute-done | bytes 557088 | tf_op jit(solution)/shard_map/ppermute | solution.py:82
  562.9 4.1 convolution_bitcast_fusion.1
  569.4 4.1 convolution_bitcast_fusion
  605.5 10.1 %collective-permute-done.39 = bf16[2,128,1536]{2,1,0:T(8,128)(2,1)} collective-permute-done((bf16[2,128,1536]{2,1,0:T(8,128)(2,1)}, bf16[2,128,1536]{2,1,0:T(8,128)(2,1)}, u32[]{:S(2)}, u32[]{:S(2)}) %collective-permute-start.39) | collective-permute-done | bytes 786464 | tf_op jit(solution)/shard_map/ppermute | solution.py:76
  616.8 6.2 bitcast_convert_fusion
  644.6 5.6 fusion.33
  652.0 13.2 %fusion.2 = f32[1024,1408]{1,0:T(8,128)} fusion(bf16[3072,1024]{1,0:T(8,128)(2,1)S(1)} %bitcast.354, s32[3072]{0:T(1024)S(1)} %fusion.116), kind=kOutput, calls=%fused_computation.3 | convolution fusion | flops 8862695424 | bytes 12070912 | tf_op jit(solution)/shard_map/dot_general | solution.py:29
  665.2 12.8 %fusion.3 = f32[1024,1408]{1,0:T(8,128)} fusion(bf16[3072,1024]{1,0:T(8,128)(2,1)S(1)} %bitcast.354, s32[1408]{0:T(1024)S(1)} %copy-done.107, s32[3072]{0:T(1024)S(1)} %fusion.116), kind=kOutput, calls=%fused_computation.4 | convolution fusion | flops 8862695424 | bytes 12076544 | tf_op jit(solution)/shard_map/dot_general | solution.py:29
  678.2 5.0 fusion.18
  684.1 4.3 collective-permute-done.53
  696.1 9.6 %collective-permute-done.58 = bf16[512,512]{1,0:T(8,128)(2,1)S(1)} collective-permute-done((bf16[512,512]{1,0:T(8,128)(2,1)S(1)}, bf16[512,512]{1,0:T(8,128)(2,1)S(1)}, u32[]{:S(2)}, u32[]{:S(2)}) %collective-permute-start.58) | collective-permute-done | bytes 524320 | tf_op jit(solution)/shard_map/ppermute | solution.py:82
  711.5 5.6 collective-permute-done.59
  717.1 3.6 collective-permute-start.46
  724.3 16.5 %collective-permute-start.55 = (f32[19,1024]{1,0:T(8,128)S(1)}, f32[19,1024]{1,0:T(8,128)S(1)}, u32[]{:S(2)}, u32[]{:S(2)}) collective-permute-start(f32[19,1024]{1,0:T(8,128)S(1)} %collective-permute-done.54), channel_id=1, source_target_pairs={{0,8},{2,10},{4,12},{6,14},{8,16},{10,18},{12,20},{14,22},{16,24},... | collective-permute-start | bytes 233480 | tf_op jit(solution)/shard_map/ppermute | solution.py:82
  740.9 3.8 collective-permute-start.64
  745.5 6.4 collective-permute-done.63
  751.9 27.8 %collective-permute-done.64 = bf16[2,128,256]{2,1,0:T(8,128)(2,1)S(1)} collective-permute-done((bf16[2,128,256]{2,1,0:T(8,128)(2,1)S(1)}, bf16[2,128,256]{2,1,0:T(8,128)(2,1)S(1)}, u32[]{:S(2)}, u32[]{:S(2)}) %collective-permute-start.64) | collective-permute-done | bytes 131104 | tf_op jit(solution)/shard_map/ppermute | solution.py:82
  784.8 4.2 collective-permute-done.66
  791.3 12.5 %collective-permute-done.48 = bf16[128,2048]{1,0:T(8,128)(2,1)S(1)} collective-permute-done((bf16[128,2048]{1,0:T(8,128)(2,1)S(1)}, bf16[128,2048]{1,0:T(8,128)(2,1)S(1)}, u32[]{:S(2)}, u32[]{:S(2)}) %collective-permute-start.48) | collective-permute-done | bytes 524320 | tf_op jit(solution)/shard_map/ppermute | solution.py:82
  808.9 86.9 %all-reduce.15.cloned.1.call-done = (bf16[1024,3072]{1,0:T(8,128)(2,1)}, bf16[1024,576]{0,1:T(8,128)(2,1)}, bf16[1024,2048]{1,0:T(8,128)(2,1)}) async-done(((bf16[1024,3072]{1,0:T(8,128)(2,1)}, bf16[1024,576]{0,1:T(8,128)(2,1)}, bf16[1024,2048]{1,0:T(8,128)(2,1)}), (bf16[1024,3072]{1,0:T(8,128)(2,1)}, bf16[1024,576]{0,1:T(8,128)(2,1)}, bf16[1024,2048]{1,0:T(8,128)(2,1)})) %all-reduce.15.cloned.1.call-update) | async-done | bytes 11665424 | tf_op jit(solution)/shard_map/psum | solution.py:906
  895.8 9.4 %convert_element_type.807 = f32[1024,3072]{1,0:T(8,128)} convert(bf16[1024,3072]{1,0:T(8,128)(2,1)} %get-tuple-element.88) | non-fusion elementwise | flops 3145728 | bytes 18874368 | tf_op jit(solution)/shard_map/convert_element_type | solution.py:952
  905.2 4.5 convert_element_type.822
  (625 shorter events, 282.3 us)
Async XLA Ops:
  7.3 172.5 %all-gather.9.cloned.1.call-start = ((), (), s32[]{:S(2)}) async-start(), calls=%async_computation.2 | async-start | bytes 18382848 | tf_op jit(solution)/shard_map/all_gather | solution.py:700
  10.8 537.4 %all-gather.7.cloned.1.call-start = ((), (), s32[]{:S(2)}) async-start(), calls=%async_computation.1 | async-start | bytes 3342336 | tf_op jit(solution)/shard_map/all_gather | solution.py:827
  11.7 20.8 %collective-permute-start = (bf16[128,1024]{1,0:T(8,128)(2,1)}, bf16[128,1024]{1,0:T(8,128)(2,1)}, u32[]{:S(2)}, u32[]{:S(2)}) collective-permute-start(bf16[128,1024]{1,0:T(8,128)(2,1)} %get-tuple-element.147), channel_id=1, source_target_pairs={{0,1},{1,0},{2,3},{3,2},{4,5},{5,4},{6,7},{7,6},{8,9},{9,8},{10,11... | collective-permute-start | bytes 786440 | tf_op jit(solution)/shard_map/ppermute | solution.py:76
  16.0 13.2 %collective-permute-start.1 = (f32[2,128]{1,0:T(2,128)S(1)}, f32[2,128]{1,0:T(2,128)}, u32[]{:S(2)}, u32[]{:S(2)}) collective-permute-start(f32[2,128]{1,0:T(2,128)S(1)} %get-tuple-element.174), channel_id=1, source_target_pairs={{0,1},{1,0},{2,3},{3,2},{4,5},{5,4},{6,7},{7,6},{8,9},{9,8},{10,11... | collective-permute-start | bytes 3080 | tf_op jit(solution)/shard_map/ppermute | solution.py:76
  16.1 15.6 %collective-permute-start.3 = (bf16[18,1024]{1,0:T(8,128)(2,1)S(1)}, bf16[18,1024]{1,0:T(8,128)(2,1)S(1)}, u32[]{:S(2)}, u32[]{:S(2)}) collective-permute-start(bf16[18,1024]{1,0:T(8,128)(2,1)S(1)} %pad_maximum_fusion.26), channel_id=1, source_target_pairs={{0,1},{1,0},{2,3},{3,2},{4,5},{5,4},{6,7},{7,6},{8,9},{9,8},{10,11... | collective-permute-start | bytes 110600 | tf_op jit(solution)/shard_map/ppermute | solution.py:76
  39.6 27.8 %collective-permute-start.4 = (bf16[2,128,1536]{2,1,0:T(8,128)(2,1)}, bf16[2,128,1536]{2,1,0:T(8,128)(2,1)}, u32[]{:S(2)}, u32[]{:S(2)}) collective-permute-start(bf16[2,128,1536]{2,1,0:T(8,128)(2,1)} %bitcast.11), channel_id=1, source_target_pairs={{0,1},{1,0},{2,3},{3,2},{4,5},{5,4},{6,7},{7,6},{8,9},{9,8},{10,11... | collective-permute-start | bytes 2359304 | tf_op jit(solution)/shard_map/ppermute | solution.py:76
  72.0 19.6 %collective-permute-start.5 = (bf16[128,2048]{1,0:T(8,128)(2,1)}, bf16[128,2048]{1,0:T(8,128)(2,1)}, u32[]{:S(2)}, u32[]{:S(2)}) collective-permute-start(bf16[128,2048]{1,0:T(8,128)(2,1)} %dynamic-slice_add_fusion), channel_id=1, source_target_pairs={{0,1},{1,0},{2,3},{3,2},{4,5},{5,4},{6,7},{7,6},{8,9},{9,8},{10,11... | collective-permute-start | bytes 1572872 | tf_op jit(solution)/shard_map/ppermute | solution.py:76
  83.6 14.6 %collective-permute-start.7 = (bf16[2,48,1024]{2,1,0:T(8,128)(2,1)S(1)}, bf16[2,48,1024]{2,1,0:T(8,128)(2,1)S(1)}, u32[]{:S(2)}, u32[]{:S(2)}) collective-permute-start(bf16[2,48,1024]{2,1,0:T(8,128)(2,1)S(1)} %fusion.104), channel_id=1, source_target_pairs={{0,1},{1,0},{2,3},{3,2},{4,5},{5,4},{6,7},{7,6},{8,9},{9,8},{10,11... | collective-permute-start | bytes 589832 | tf_op jit(solution)/shard_map/ppermute | solution.py:76
  140.2 15.5 %collective-permute-start.9 = (bf16[64,2048]{1,0:T(8,128)(2,1)}, bf16[64,2048]{1,0:T(8,128)(2,1)}, u32[]{:S(2)}, u32[]{:S(2)}) collective-permute-start(bf16[64,2048]{1,0:T(8,128)(2,1)} %get-tuple-element.145), channel_id=1, source_target_pairs={{0,8},{2,10},{4,12},{6,14},{8,16},{10,18},{12,20},{14,22},{16,24},... | collective-permute-start | bytes 786440 | tf_op jit(solution)/shard_map/ppermute | solution.py:82
  175.4 31.9 %collective-permute-start.17 = (bf16[4,64,2048]{2,1,0:T(8,128)(2,1)}, bf16[4,64,2048]{2,1,0:T(8,128)(2,1)}, u32[]{:S(2)}, u32[]{:S(2)}) collective-permute-start(bf16[4,64,2048]{2,1,0:T(8,128)(2,1)} %get-tuple-element.126), channel_id=1, source_target_pairs={{0,1},{1,0},{2,3},{3,2},{4,5},{5,4},{6,7},{7,6},{8,9},{9,8},{10,11... | collective-permute-start | bytes 3145736 | tf_op jit(solution)/shard_map/ppermute | solution.py:76
  178.4 31.8 %collective-permute-start.12 = (bf16[4,64,2048]{2,1,0:T(8,128)(2,1)}, bf16[4,64,2048]{2,1,0:T(8,128)(2,1)}, u32[]{:S(2)}, u32[]{:S(2)}) collective-permute-start(bf16[4,64,2048]{2,1,0:T(8,128)(2,1)} %get-tuple-element.128), channel_id=1, source_target_pairs={{0,4},{2,6},{4,0},{6,2},{8,12},{10,14},{12,8},{14,10},{16,20},{18,... | collective-permute-start | bytes 3145736 | tf_op jit(solution)/shard_map/ppermute | solution.py:82
  216.5 47.9 %collective-permute-start.22 = (bf16[2,4,64,2048]{3,2,1,0:T(8,128)(2,1)}, bf16[2,4,64,2048]{3,2,1,0:T(8,128)(2,1)S(1)}, u32[]{:S(2)}, u32[]{:S(2)}) collective-permute-start(bf16[2,4,64,2048]{3,2,1,0:T(8,128)(2,1)} %pad_maximum_fusion.1.refs_2_), channel_id=1, source_target_pairs={{0,4},{2,6},{4,0},{6,2},{8,12},{10,14},{12,8},{14,10},{16,20},{18,... | collective-permute-start | bytes 6291464 | tf_op jit(solution)/shard_map/ppermute | solution.py:82
  217.2 47.7 %collective-permute-start.20 = (bf16[2,4,64,2048]{3,2,1,0:T(8,128)(2,1)}, bf16[2,4,64,2048]{3,2,1,0:T(8,128)(2,1)S(1)}, u32[]{:S(2)}, u32[]{:S(2)}) collective-permute-start(bf16[2,4,64,2048]{3,2,1,0:T(8,128)(2,1)} %pad_maximum_fusion.refs_0_), channel_id=1, source_target_pairs={{0,1},{1,0},{2,3},{3,2},{4,5},{5,4},{6,7},{7,6},{8,9},{9,8},{10,11... | collective-permute-start | bytes 6291464 | tf_op jit(solution)/shard_map/ppermute | solution.py:76
  316.5 65.0 %collective-permute-start.19 = (bf16[2,4,64,2176]{3,2,1,0:T(8,128)(2,1)}, bf16[2,4,64,2176]{3,2,1,0:T(8,128)(2,1)S(1)}, u32[]{:S(2)}, u32[]{:S(2)}) collective-permute-start(bf16[2,4,64,2176]{3,2,1,0:T(8,128)(2,1)} %get-tuple-element.52), channel_id=1, source_target_pairs={{0,2},{2,0},{4,6},{6,4},{8,10},{10,8},{12,14},{14,12},{16,18},{18,... | collective-permute-start | bytes 6684680 | tf_op jit(solution)/shard_map/ppermute | solution.py:82
  316.7 72.6 %collective-permute-start.28 = (bf16[2,4,64,2176]{3,2,1,0:T(8,128)(2,1)}, bf16[2,4,64,2176]{3,2,1,0:T(8,128)(2,1)}, u32[]{:S(2)}, u32[]{:S(2)}) collective-permute-start(bf16[2,4,64,2176]{3,2,1,0:T(8,128)(2,1)} %get-tuple-element.67), channel_id=1, source_target_pairs={{0,2},{2,0},{4,6},{6,4},{8,10},{10,8},{12,14},{14,12},{16,18},{18,... | collective-permute-start | bytes 6684680 | tf_op jit(solution)/shard_map/ppermute | solution.py:82
  325.5 56.0 %collective-permute-start.25 = (bf16[2,4,64,2176]{3,2,1,0:T(8,128)(2,1)}, bf16[2,4,64,2176]{3,2,1,0:T(8,128)(2,1)}, u32[]{:S(2)}, u32[]{:S(2)}) collective-permute-start(bf16[2,4,64,2176]{3,2,1,0:T(8,128)(2,1)} %add_convert_fusion.5), channel_id=1, source_target_pairs={{0,1},{1,0},{2,3},{3,2},{4,5},{5,4},{6,7},{7,6},{8,9},{9,8},{10,11... | collective-permute-start | bytes 6684680 | tf_op jit(solution)/shard_map/ppermute | solution.py:76
  330.1 59.2 %collective-permute-start.29 = (bf16[2,4,64,2176]{3,2,1,0:T(8,128)(2,1)}, bf16[2,4,64,2176]{3,2,1,0:T(8,128)(2,1)}, u32[]{:S(2)}, u32[]{:S(2)}) collective-permute-start(bf16[2,4,64,2176]{3,2,1,0:T(8,128)(2,1)} %add_convert_fusion.4), channel_id=1, source_target_pairs={{0,4},{2,6},{4,0},{6,2},{8,12},{10,14},{12,8},{14,10},{16,20},{18,... | collective-permute-start | bytes 6684680 | tf_op jit(solution)/shard_map/ppermute | solution.py:82
  418.7 135.1 %all-gather.5.cloned.1.call-start = ((), (), s32[]{:S(2)}) async-start(), calls=%async_computation | async-start | bytes 6684672 | tf_op jit(solution)/shard_map/all_gather | solution.py:826
  418.8 30.5 %collective-permute-start.27 = (bf16[4,64,2176]{2,1,0:T(8,128)(2,1)}, bf16[4,64,2176]{2,1,0:T(8,128)(2,1)}, u32[]{:S(2)}, u32[]{:S(2)}) collective-permute-start(bf16[4,64,2176]{2,1,0:T(8,128)(2,1)} %copy-done.51), channel_id=1, source_target_pairs={{0,4},{2,6},{4,0},{6,2},{8,12},{10,14},{12,8},{14,10},{16,20},{18,... | collective-permute-start | bytes 3342344 | tf_op jit(solution)/shard_map/ppermute | solution.py:82
  429.8 25.4 %collective-permute-start.32 = (bf16[4,64,2176]{2,1,0:T(8,128)(2,1)}, bf16[4,64,2176]{2,1,0:T(8,128)(2,1)S(1)}, u32[]{:S(2)}, u32[]{:S(2)}) collective-permute-start(bf16[4,64,2176]{2,1,0:T(8,128)(2,1)} %copy-done.52), channel_id=1, source_target_pairs={{0,1},{1,0},{2,3},{3,2},{4,5},{5,4},{6,7},{7,6},{8,9},{9,8},{10,11... | collective-permute-start | bytes 3342344 | tf_op jit(solution)/shard_map/ppermute | solution.py:76
  456.5 18.6 %collective-permute-start.33 = (bf16[128,2176]{1,0:T(8,128)(2,1)S(1)}, bf16[128,2176]{1,0:T(8,128)(2,1)S(1)}, u32[]{:S(2)}, u32[]{:S(2)}) collective-permute-start(bf16[128,2176]{1,0:T(8,128)(2,1)S(1)} %pad_maximum_fusion.11), channel_id=1, source_target_pairs={{0,8},{2,10},{4,12},{6,14},{8,16},{10,18},{12,20},{14,22},{16,24},... | collective-permute-start | bytes 1671176 | tf_op jit(solution)/shard_map/ppermute | solution.py:82
  472.1 33.8 %collective-permute-start.30 = (bf16[2,4,64,2048]{3,2,1,0:T(8,128)(2,1)}, bf16[2,4,64,2048]{3,2,1,0:T(8,128)(2,1)}, u32[]{:S(2)}, u32[]{:S(2)}) collective-permute-start(bf16[2,4,64,2048]{3,2,1,0:T(8,128)(2,1)} %get-tuple-element.72), channel_id=1, source_target_pairs={{0,2},{2,0},{4,6},{6,4},{8,10},{10,8},{12,14},{14,12},{16,18},{18,... | collective-permute-start | bytes 6291464 | tf_op jit(solution)/shard_map/ppermute | solution.py:82
  477.2 27.4 %collective-permute-start.34 = (bf16[128,2176]{1,0:T(8,128)(2,1)}, bf16[128,2176]{1,0:T(8,128)(2,1)}, u32[]{:S(2)}, u32[]{:S(2)}) collective-permute-start(bf16[128,2176]{1,0:T(8,128)(2,1)} %add_convert_fusion.17), channel_id=1, source_target_pairs={{0,8},{2,10},{4,12},{6,14},{8,16},{10,18},{12,20},{14,22},{16,24},... | collective-permute-start | bytes 1671176 | tf_op jit(solution)/shard_map/ppermute | solution.py:82
  494.0 19.1 %collective-permute-start.36 = (bf16[2,4,64,2048]{3,2,1,0:T(8,128)(2,1)}, bf16[2,4,64,2048]{3,2,1,0:T(8,128)(2,1)}, u32[]{:S(2)}, u32[]{:S(2)}) collective-permute-start(bf16[2,4,64,2048]{3,2,1,0:T(8,128)(2,1)} %get-tuple-element.74), channel_id=1, source_target_pairs={{0,2},{2,0},{4,6},{6,4},{8,10},{10,8},{12,14},{14,12},{16,18},{18,... | collective-permute-start | bytes 6291464 | tf_op jit(solution)/shard_map/ppermute | solution.py:82
  495.7 142.7 %collective-permute-start.42 = (bf16[2,4,64,2048]{3,2,1,0:T(8,128)(2,1)}, bf16[2,4,64,2048]{3,2,1,0:T(8,128)(2,1)}, u32[]{:S(2)}, u32[]{:S(2)}) collective-permute-start(bf16[2,4,64,2048]{3,2,1,0:T(8,128)(2,1)} %get-tuple-element.76), channel_id=1, source_target_pairs={{0,2},{2,0},{4,6},{6,4},{8,10},{10,8},{12,14},{14,12},{16,18},{18,... | collective-permute-start | bytes 6291464 | tf_op jit(solution)/shard_map/ppermute | solution.py:82
  498.7 37.6 %collective-permute-start.43 = (bf16[2,4,64,2048]{3,2,1,0:T(8,128)(2,1)}, bf16[2,4,64,2048]{3,2,1,0:T(8,128)(2,1)S(1)}, u32[]{:S(2)}, u32[]{:S(2)}) collective-permute-start(bf16[2,4,64,2048]{3,2,1,0:T(8,128)(2,1)} %get-tuple-element.78), channel_id=1, source_target_pairs={{0,2},{2,0},{4,6},{6,4},{8,10},{10,8},{12,14},{14,12},{16,18},{18,... | collective-permute-start | bytes 6291464 | tf_op jit(solution)/shard_map/ppermute | solution.py:82
  505.9 24.9 %collective-permute-start.35 = (bf16[128,2176]{1,0:T(8,128)(2,1)S(1)}, bf16[128,2176]{1,0:T(8,128)(2,1)S(1)}, u32[]{:S(2)}, u32[]{:S(2)}) collective-permute-start(bf16[128,2176]{1,0:T(8,128)(2,1)S(1)} %add_convert_fusion.16), channel_id=1, source_target_pairs={{0,8},{2,10},{4,12},{6,14},{8,16},{10,18},{12,20},{14,22},{16,24},... | collective-permute-start | bytes 1671176 | tf_op jit(solution)/shard_map/ppermute | solution.py:82
  512.1 181.6 %collective-permute-start.31 = (bf16[4,64,2048]{2,1,0:T(8,128)(2,1)}, bf16[4,64,2048]{2,1,0:T(8,128)(2,1)}, u32[]{:S(2)}, u32[]{:S(2)}) collective-permute-start(bf16[4,64,2048]{2,1,0:T(8,128)(2,1)} %slice_bitcast_fusion.8), channel_id=1, source_target_pairs={{0,4},{2,6},{4,0},{6,2},{8,12},{10,14},{12,8},{14,10},{16,20},{18,... | collective-permute-start | bytes 3145736 | tf_op jit(solution)/shard_map/ppermute | solution.py:82
  536.3 99.0 %collective-permute-start.40 = (bf16[4,64,2048]{2,1,0:T(8,128)(2,1)}, bf16[4,64,2048]{2,1,0:T(8,128)(2,1)}, u32[]{:S(2)}, u32[]{:S(2)}) collective-permute-start(bf16[4,64,2048]{2,1,0:T(8,128)(2,1)} %slice_bitcast_fusion.6), channel_id=1, source_target_pairs={{0,4},{2,6},{4,0},{6,2},{8,12},{10,14},{12,8},{14,10},{16,20},{18,... | collective-permute-start | bytes 3145736 | tf_op jit(solution)/shard_map/ppermute | solution.py:82
  538.5 101.3 %collective-permute-start.44 = (bf16[2,4,64,2048]{3,2,1,0:T(8,128)(2,1)}, bf16[2,4,64,2048]{3,2,1,0:T(8,128)(2,1)}, u32[]{:S(2)}, u32[]{:S(2)}) collective-permute-start(bf16[2,4,64,2048]{3,2,1,0:T(8,128)(2,1)} %add_convert_fusion.9), channel_id=1, source_target_pairs={{0,4},{2,6},{4,0},{6,2},{8,12},{10,14},{12,8},{14,10},{16,20},{18,... | collective-permute-start | bytes 6291464 | tf_op jit(solution)/shard_map/ppermute | solution.py:82
  595.9 19.7 %collective-permute-start.39 = (bf16[2,128,1536]{2,1,0:T(8,128)(2,1)}, bf16[2,128,1536]{2,1,0:T(8,128)(2,1)}, u32[]{:S(2)}, u32[]{:S(2)}) collective-permute-start(bf16[2,128,1536]{2,1,0:T(8,128)(2,1)} %copy.215), channel_id=1, source_target_pairs={{0,1},{1,0},{2,3},{3,2},{4,5},{5,4},{6,7},{7,6},{8,9},{9,8},{10,11... | collective-permute-start | bytes 2359304 | tf_op jit(solution)/shard_map/ppermute | solution.py:76
  624.2 271.6 %all-reduce.15.cloned.1.call-start = ((), (), s32[]{:S(2)}) async-start(), calls=%async_computation.3 | async-start | bytes 23330816 | tf_op jit(solution)/shard_map/psum | solution.py:906
  629.9 59.1 %collective-permute-start.57 = (bf16[1024,512]{1,0:T(8,128)(2,1)}, bf16[1024,512]{1,0:T(8,128)(2,1)}, u32[]{:S(2)}, u32[]{:S(2)}) collective-permute-start(bf16[1024,512]{1,0:T(8,128)(2,1)} %constant_dynamic-slice_fusion.6), channel_id=1, source_target_pairs={{0,2},{2,0},{4,6},{6,4},{8,10},{10,8},{12,14},{14,12},{16,18},{18,... | collective-permute-start | bytes 3145736 | tf_op jit(solution)/shard_map/ppermute | solution.py:82
  635.3 42.7 %collective-permute-start.51 = (f32[17,1024]{1,0:T(8,128)S(1)}, f32[17,1024]{1,0:T(8,128)S(1)}, u32[]{:S(2)}, u32[]{:S(2)}) collective-permute-start(f32[17,1024]{1,0:T(8,128)S(1)} %pad_maximum_fusion.20), channel_id=1, source_target_pairs={{0,1},{1,0},{2,3},{3,2},{4,5},{5,4},{6,7},{7,6},{8,9},{9,8},{10,11... | collective-permute-start | bytes 208904 | tf_op jit(solution)/shard_map/ppermute | solution.py:76
  638.4 55.3 %collective-permute-start.41 = (bf16[4,64,2048]{2,1,0:T(8,128)(2,1)S(1)}, bf16[4,64,2048]{2,1,0:T(8,128)(2,1)S(1)}, u32[]{:S(2)}, u32[]{:S(2)}) collective-permute-start(bf16[4,64,2048]{2,1,0:T(8,128)(2,1)S(1)} %fusion.20), channel_id=1, source_target_pairs={{0,1},{1,0},{2,3},{3,2},{4,5},{5,4},{6,7},{7,6},{8,9},{9,8},{10,11... | collective-permute-start | bytes 3145736 | tf_op jit(solution)/shard_map/ppermute | solution.py:76
  643.4 49.1 %collective-permute-start.45 = (bf16[4,64,2048]{2,1,0:T(8,128)(2,1)S(1)}, bf16[4,64,2048]{2,1,0:T(8,128)(2,1)S(1)}, u32[]{:S(2)}, u32[]{:S(2)}) collective-permute-start(bf16[4,64,2048]{2,1,0:T(8,128)(2,1)S(1)} %slice_bitcast_fusion.4), channel_id=1, source_target_pairs={{0,1},{1,0},{2,3},{3,2},{4,5},{5,4},{6,7},{7,6},{8,9},{9,8},{10,11... | collective-permute-start | bytes 3145736 | tf_op jit(solution)/shard_map/ppermute | solution.py:76
  688.5 35.5 %collective-permute-start.50 = (bf16[128,1024]{1,0:T(8,128)(2,1)S(1)}, bf16[128,1024]{1,0:T(8,128)(2,1)S(1)}, u32[]{:S(2)}, u32[]{:S(2)}) collective-permute-start(bf16[128,1024]{1,0:T(8,128)(2,1)S(1)} %get-tuple-element.138), channel_id=1, source_target_pairs={{0,1},{1,0},{2,3},{3,2},{4,5},{5,4},{6,7},{7,6},{8,9},{9,8},{10,11... | collective-permute-start | bytes 786440 | tf_op jit(solution)/shard_map/ppermute | solution.py:76
  689.0 35.3 %collective-permute-start.54 = (f32[19,1024]{1,0:T(8,128)S(1)}, f32[19,1024]{1,0:T(8,128)S(1)}, u32[]{:S(2)}, u32[]{:S(2)}) collective-permute-start(f32[19,1024]{1,0:T(8,128)S(1)} %add.1024), channel_id=1, source_target_pairs={{0,8},{2,10},{4,12},{6,14},{8,16},{10,18},{12,20},{14,22},{16,24},... | collective-permute-start | bytes 233480 | tf_op jit(solution)/shard_map/ppermute | solution.py:82
  707.4 15.0 %collective-permute-start.60 = (bf16[128,512]{1,0:T(8,128)(2,1)S(1)}, bf16[128,512]{1,0:T(8,128)(2,1)S(1)}, u32[]{:S(2)}, u32[]{:S(2)}) collective-permute-start(bf16[128,512]{1,0:T(8,128)(2,1)S(1)} %get-tuple-element.137), channel_id=1, source_target_pairs={{0,16},{2,18},{4,20},{6,22},{8,24},{10,26},{12,28},{14,30},{16,0},... | collective-permute-start | bytes 393224 | tf_op jit(solution)/shard_map/ppermute | solution.py:82
  708.8 13.5 %collective-permute-start.61 = (bf16[128,512]{1,0:T(8,128)(2,1)S(1)}, bf16[128,512]{1,0:T(8,128)(2,1)S(1)}, u32[]{:S(2)}, u32[]{:S(2)}) collective-permute-start(bf16[128,512]{1,0:T(8,128)(2,1)S(1)} %get-tuple-element.136), channel_id=1, source_target_pairs={{0,24},{2,26},{4,28},{6,30},{8,0},{10,2},{12,4},{14,6},{16,8},{18,... | collective-permute-start | bytes 393224 | tf_op jit(solution)/shard_map/ppermute | solution.py:82
  717.1 27.7 %collective-permute-start.46 = (bf16[128,2048]{1,0:T(8,128)(2,1)S(1)}, bf16[128,2048]{1,0:T(8,128)(2,1)S(1)}, u32[]{:S(2)}, u32[]{:S(2)}) collective-permute-start(bf16[128,2048]{1,0:T(8,128)(2,1)S(1)} %pad_maximum_fusion.13), channel_id=1, source_target_pairs={{0,8},{2,10},{4,12},{6,14},{8,16},{10,18},{12,20},{14,22},{16,24},... | collective-permute-start | bytes 1572872 | tf_op jit(solution)/shard_map/ppermute | solution.py:82
  722.5 18.3 %collective-permute-start.62 = (bf16[128,256]{1,0:T(8,128)(2,1)S(1)}, bf16[128,256]{1,0:T(8,128)(2,1)S(1)}, u32[]{:S(2)}, u32[]{:S(2)}) collective-permute-start(bf16[128,256]{1,0:T(8,128)(2,1)S(1)} %get-tuple-element.156), channel_id=1, source_target_pairs={{0,1},{1,0},{2,3},{3,2},{4,5},{5,4},{6,7},{7,6},{8,9},{9,8},{10,11... | collective-permute-start | bytes 196616 | tf_op jit(solution)/shard_map/ppermute | solution.py:76
  724.3 57.1 %collective-permute-start.55 = (f32[19,1024]{1,0:T(8,128)S(1)}, f32[19,1024]{1,0:T(8,128)S(1)}, u32[]{:S(2)}, u32[]{:S(2)}) collective-permute-start(f32[19,1024]{1,0:T(8,128)S(1)} %collective-permute-done.54), channel_id=1, source_target_pairs={{0,8},{2,10},{4,12},{6,14},{8,16},{10,18},{12,20},{14,22},{16,24},... | collective-permute-start | bytes 233480 | tf_op jit(solution)/shard_map/ppermute | solution.py:82
  740.9 38.7 %collective-permute-start.64 = (bf16[2,128,256]{2,1,0:T(8,128)(2,1)S(1)}, bf16[2,128,256]{2,1,0:T(8,128)(2,1)S(1)}, u32[]{:S(2)}, u32[]{:S(2)}) collective-permute-start(bf16[2,128,256]{2,1,0:T(8,128)(2,1)S(1)} %get-tuple-element.92), channel_id=1, source_target_pairs={{0,16},{2,18},{4,20},{6,22},{8,24},{10,26},{12,28},{14,30},{16,0},... | collective-permute-start | bytes 393224 | tf_op jit(solution)/shard_map/ppermute | solution.py:82
  744.9 37.3 %collective-permute-start.47 = (bf16[128,2048]{1,0:T(8,128)(2,1)S(1)}, bf16[128,2048]{1,0:T(8,128)(2,1)S(1)}, u32[]{:S(2)}, u32[]{:S(2)}) collective-permute-start(bf16[128,2048]{1,0:T(8,128)(2,1)S(1)} %add_convert_fusion.22), channel_id=1, source_target_pairs={{0,8},{2,10},{4,12},{6,14},{8,16},{10,18},{12,20},{14,22},{16,24},... | collective-permute-start | bytes 1572872 | tf_op jit(solution)/shard_map/ppermute | solution.py:82
  744.9 34.7 %collective-permute-start.65 = (bf16[2,128,256]{2,1,0:T(8,128)(2,1)S(1)}, bf16[2,128,256]{2,1,0:T(8,128)(2,1)S(1)}, u32[]{:S(2)}, u32[]{:S(2)}) collective-permute-start(bf16[2,128,256]{2,1,0:T(8,128)(2,1)S(1)} %get-tuple-element.92), channel_id=1, source_target_pairs={{0,8},{2,10},{4,12},{6,14},{8,16},{10,18},{12,20},{14,22},{16,24},... | collective-permute-start | bytes 393224 | tf_op jit(solution)/shard_map/ppermute | solution.py:82
  782.3 21.4 %collective-permute-start.48 = (bf16[128,2048]{1,0:T(8,128)(2,1)S(1)}, bf16[128,2048]{1,0:T(8,128)(2,1)S(1)}, u32[]{:S(2)}, u32[]{:S(2)}) collective-permute-start(bf16[128,2048]{1,0:T(8,128)(2,1)S(1)} %add_convert_fusion.21), channel_id=1, source_target_pairs={{0,8},{2,10},{4,12},{6,14},{8,16},{10,18},{12,20},{14,22},{16,24},... | collective-permute-start | bytes 1572872 | tf_op jit(solution)/shard_map/ppermute | solution.py:82
  789.3 16.2 %collective-permute-start.67 = (bf16[2,1024,256]{2,1,0:T(8,128)(2,1)S(1)}, bf16[2,1024,256]{2,1,0:T(8,128)(2,1)S(1)}, u32[]{:S(2)}, u32[]{:S(2)}) collective-permute-start(bf16[2,1024,256]{2,1,0:T(8,128)(2,1)S(1)} %maximum_select_fusion.7), channel_id=1, source_target_pairs={{0,2},{2,0},{4,6},{6,4},{8,10},{10,8},{12,14},{14,12},{16,18},{18,... | collective-permute-start | bytes 3145736 | tf_op jit(solution)/shard_map/ppermute | solution.py:82
  (156 other events, 1604.0 us)
Sparse Core Ops, SparseCore 0:
  11.5 133.2 all-gather.8
  418.9 49.4 all-gather.6
  470.7 83.0 all-gather.4
  630.1 265.6 all-reduce.14
